TPU v7x, 32 devices: a whole 2x2x4 slice. The times are simulated.
32 devices in a mesh: ja: 4 (over x, core), ka: 8 (over z, y).
Axes of the slice: x: 2, y: 2, z: 4, core: 2. Of those that a mesh axis runs over, the one named last changes fastest.
Arguments:
- blocks: bfloat16 [1024, 64, 4096], P(('ja', 'ka')), may hold values from -6 to 6
- factor_b: bfloat16 [2048, 256], P('ja'), may hold values from -0.3984375 to 0.3984375
- factor_c: bfloat16 [2048, 256], P('ka'), may hold values from -0.3984375 to 0.3984375
- block_coords: int32 [1024, 3], P(('ja', 'ka')), may hold values from 0 to 31, as said below
- block_count: int32 [32], P(('ja', 'ka')), may hold values from 1 to 31, as said below
Outputs:
- new_factor: float32 [2048, 256], P(('ja', 'ka'))
Inputs may be any that keep to these rules, and one draw needn't show every extreme that they name: `block_coords`: column 0 lies in 0 to 1 * 32 - 1 and is different for every slot of one device, column 1 in 0 to 7, column 2 in 0 to 3. `block_count`: a device and the device whose ka index lies half the ka axis away hold 32 live slots together; a device's live slots are its first ones.
All inputs are finite; a program needn't handle non-finite values.
Results may differ from a plain program's by a relative error of at most 0.0041.
Values may be sent and summed in bfloat16 or wider, within the bound.
No kernel may reach another device: no remote copies, remote signals or barrier semaphores. Data moves between devices by JAX's collectives and lax.ppermute only.
A program may use at most 128 MiB of HBM per device.

v0:
```python
import functools

import jax
import jax.numpy as jnp
from jax import lax
from jax.experimental import pallas as pl
from jax.experimental.pallas import tpu as pltpu
from jax.sharding import PartitionSpec as P

ALL = ("ja", "ka")
CODE_ROWS = 8
AHEAD = 4
GROUP = 8
RIDGE = 0.1
TOLERANCE = 1e-6
FIXED_STEPS = 6
MOST_STEPS = 600
MIB = 1 << 20


def xor_permute(value, mask):
    count = lax.axis_size(ALL)
    return lax.ppermute(value, ALL, [(i, i ^ mask) for i in range(count)])


def stage_plan(size_ja, size_ka):
    low = size_ka.bit_length() - 1
    core = low
    rest = [low + 1 + i for i in range(size_ja.bit_length() - 2)] + list(range(low))
    return [[core]] + [rest[i : i + 2] for i in range(0, len(rest), 2)]


def terms_kernel(
    order,
    coords_hbm,
    count,
    me,
    blocks,
    b_hbm,
    c_hbm,
    keep_ref,
    send_ref,
    held,
    b_ref,
    c_ref,
    sems,
    factor_sems,
    coords,
    waiting,
    first,
    second,
):
    edge, rank = c_ref.shape[1:]
    third_dev = c_ref.shape[0]
    half = keep_ref.shape[0]
    live = count[0]
    device = me[0]

    def fetch(slot):
        return pltpu.make_async_copy(blocks.at[slot], held.at[slot], sems.at[slot])

    factors = [
        pltpu.make_async_copy(source, place, factor_sems.at[index])
        for index, (source, place) in enumerate(((coords_hbm, coords), (b_hbm, b_ref), (c_hbm, c_ref)))
    ]
    for copy in factors:
        copy.start()
    fetch(0).start()

    for cell in range(waiting.shape[0]):
        waiting[cell] = -1
    factors[0].wait()

    def assign(slot, passes):
        cell = coords[1, slot] * third_dev + coords[2, slot]
        opened = waiting[cell]
        joins = opened >= 0
        place = jnp.where(joins, opened, passes)
        first[place] = jnp.where(joins, first[place], slot)
        second[place] = slot
        waiting[cell] = jnp.where(joins, -1, passes)
        return jnp.where(joins, passes, passes + 1)

    passes = lax.fori_loop(0, live, assign, 0)

    def fetch_pass(index):
        one, two = first[index], second[index]

        @pl.when(one > 0)
        def _():
            fetch(one).start()

        @pl.when(one != two)
        def _():
            fetch(two).start()

    for index in range(AHEAD):

        @pl.when(index < passes)
        def _():
            fetch_pass(index)

    keep_ref[...] = jnp.zeros_like(keep_ref)
    send_ref[...] = jnp.zeros_like(send_ref)
    for copy in factors[1:]:
        copy.wait()
    lanes = lax.broadcasted_iota(jnp.int32, (CODE_ROWS, rank), 1)

    def put(slot, code, term):
        relative = jnp.bitwise_xor(coords[0, slot], device)
        target = 0
        for new_bit, old_bit in enumerate(order):
            target += (lax.shift_right_logical(relative, old_bit) & 1) << new_bit
        row_code = jnp.where(lanes == relative, code, 0.0).astype(jnp.bfloat16)

        @pl.when(target < half)
        def _():
            keep_ref[target, :edge] = term
            keep_ref[target, edge:] = row_code

        @pl.when(target >= half)
        def _():
            send_ref[target - half, :edge] = term
            send_ref[target - half, edge:] = row_code

    def step(index, carry):
        @pl.when(index + AHEAD < passes)
        def _():
            fetch_pass(index + AHEAD)

        one, two = first[index], second[index]
        fetch(one).wait()

        @pl.when(one != two)
        def _():
            fetch(two).wait()

        b_index, c_index = coords[1, one], coords[2, one]
        b_rows = b_ref[b_index].astype(jnp.float32)
        c_rows = c_ref[c_index]
        total = jnp.zeros((2 * edge, rank), jnp.float32)
        for start in range(0, edge, GROUP):
            pieces = []
            for row in range(start, start + GROUP):
                spread = jnp.broadcast_to(b_rows[row : row + 1], (16, rank)).astype(jnp.bfloat16)
                for low in range(0, edge, 16):
                    pieces.append(spread * c_rows[low : low + 16])
            khatri = jnp.concatenate(pieces, axis=0)
            columns = slice(start * edge, (start + GROUP) * edge)
            part = jnp.concatenate([held[one, :, columns], held[two, :, columns]], axis=0)
            total += jnp.dot(part, khatri, preferred_element_type=jnp.float32)
        term = total.astype(jnp.bfloat16)
        code = (b_index * third_dev + c_index + 1).astype(jnp.float32)
        put(one, code, term[:edge])
        put(two, code, term[edge:])
        return carry

    lax.fori_loop(0, passes, step, 0)


def own_terms(order, blocks, b_blocks, c_blocks, coords, count, me, total_rows):
    slots, edge, width = blocks.shape
    rank = b_blocks.shape[2]
    half = jax.ShapeDtypeStruct((total_rows // 2, edge + CODE_ROWS, rank), jnp.bfloat16)
    smem = pl.BlockSpec(memory_space=pltpu.SMEM)
    vmem = pl.BlockSpec(memory_space=pltpu.VMEM)
    hbm = pl.BlockSpec(memory_space=pltpu.HBM)
    in_hbm = functools.partial(pltpu.with_memory_space_constraint, memory_space=pltpu.HBM)
    return pl.pallas_call(
        functools.partial(terms_kernel, order),
        out_shape=(half, half),
        in_specs=[hbm, smem, smem, hbm, hbm, hbm],
        out_specs=(vmem, vmem),
        scratch_shapes=[
            pltpu.VMEM((slots, edge, width), blocks.dtype),
            pltpu.VMEM(b_blocks.shape, b_blocks.dtype),
            pltpu.VMEM(c_blocks.shape, c_blocks.dtype),
            pltpu.SemaphoreType.DMA((slots,)),
            pltpu.SemaphoreType.DMA((3,)),
            pltpu.SMEM((3, slots), jnp.int32),
            pltpu.SMEM((b_blocks.shape[0] * c_blocks.shape[0],), jnp.int32),
            pltpu.SMEM((slots,), jnp.int32),
            pltpu.SMEM((slots,), jnp.int32),
        ],
        compiler_params=pltpu.CompilerParams(vmem_limit_bytes=52 * MIB),
        cost_estimate=pl.CostEstimate(
            flops=slots * edge * width * rank * 2,
            bytes_accessed=slots * edge * width * 2,
            transcendentals=0,
        ),
        name="own_terms",
    )(in_hbm(coords.T), count, me, blocks, in_hbm(b_blocks), in_hbm(c_blocks))


def grams_kernel(*refs):
    gram_ref = refs[-1]
    edge = refs[0].shape[1]
    place = 0
    for ref in refs[:-1]:
        for block in range(ref.shape[0]):
            rows = ref[block]
            gram_ref[place] = lax.dot_general(
                rows, rows, (((0,), (0,)), ((), ())), preferred_element_type=jnp.float32
            )
            place += 1
    del edge


def grams_of(parts):
    rank = parts[0].shape[2]
    edge = parts[0].shape[1]
    number = sum(p.shape[0] for p in parts)
    vmem = pl.BlockSpec(memory_space=pltpu.VMEM)
    return pl.pallas_call(
        grams_kernel,
        out_shape=jax.ShapeDtypeStruct((number, rank, rank), jnp.float32),
        in_specs=[vmem] * len(parts),
        out_specs=vmem,
        compiler_params=pltpu.CompilerParams(vmem_limit_bytes=(number * rank * rank * 4 + 6 * MIB)),
        cost_estimate=pl.CostEstimate(
            flops=number * edge * rank * rank * 2,
            bytes_accessed=number * edge * rank * 2,
            transcendentals=0,
        ),
        name="grams",
    )(*parts)


def split3(value):
    high = value.astype(jnp.bfloat16)
    rest = value - high.astype(jnp.float32)
    middle = rest.astype(jnp.bfloat16)
    return high, middle, (rest - middle.astype(jnp.float32)).astype(jnp.bfloat16)


def solve_kernel(shape, me, moment_ref, gram_b, gram_c, out_ref, system, parts, work, b_list, c_list):
    size_ja, size_ka, second_dev, third_dev, b_place, c_place = shape
    edge, rank = out_ref.shape
    sources = size_ja * size_ka
    lanes = lax.broadcasted_iota(jnp.int32, (1, rank), 1)
    core = me[1]

    width = (second_dev * third_dev).bit_length()
    per = 24 // width
    weight = jnp.left_shift(1, width * lax.rem(lanes, per)).astype(jnp.float32)
    weighted = moment_ref[edge : edge + 1, :] * weight
    packed = [
        jnp.sum(jnp.where(lax.div(lanes, per) == group, weighted, 0.0)).astype(jnp.int32)
        for group in range(pl.cdiv(sources, per))
    ]
    half = third_dev // 2
    live = 0
    for source in range(sources):
        code = lax.shift_right_logical(packed[source // per], width * (source % per)) & ((1 << width) - 1)
        cell = jnp.maximum(code - 1, 0)
        second, third = lax.div(cell, third_dev), lax.rem(cell, third_dev)
        far = jnp.bitwise_xor(lax.div(third, half), core)
        b_list[live] = b_place[source // size_ka] * second_dev + second
        c_list[live] = (far * size_ka + c_place[source % size_ka]) * half + lax.rem(third, half)
        live = live + (code > 0).astype(jnp.int32)

    strip = min(64, rank)
    for low in range(0, rank, strip):
        rows = lax.broadcasted_iota(jnp.int32, (strip, rank), 0) + low
        columns = lax.broadcasted_iota(jnp.int32, (strip, rank), 1)

        def add(index, total, low=low):
            left = gram_b[b_list[index], low : low + strip, :]
            return total + left * gram_c[c_list[index], low : low + strip, :]

        total = lax.fori_loop(0, live, add, jnp.where(rows == columns, RIDGE, 0.0))
        system[low : low + strip] = total
        for place, part in enumerate(split3(total)):
            parts[place, low : low + strip] = part

    eye = lax.broadcasted_iota(jnp.int32, (rank, rank), 0) == lax.broadcasted_iota(jnp.int32, (rank, rank), 1)
    inverse = 1.0 / jnp.sum(jnp.where(eye, system[...], 0.0), axis=0, keepdims=True)
    moment = moment_ref[:edge, :]
    scale = jnp.max(jnp.abs(moment), axis=1, keepdims=True)
    goal = moment / jnp.where(scale > 0, scale, 1.0)
    limit = TOLERANCE * TOLERANCE * jnp.sum(goal * goal, axis=1, keepdims=True)

    def times_system(value):
        high, middle, low = split3(value)
        three = jnp.dot(
            jnp.concatenate([high, middle, low], axis=0), parts[0], preferred_element_type=jnp.float32
        )
        two = jnp.dot(jnp.concatenate([high, middle], axis=0), parts[1], preferred_element_type=jnp.float32)
        one = jnp.dot(high, parts[2], preferred_element_type=jnp.float32)
        small = (one + two[edge:]) + three[2 * edge :]
        return three[:edge] + ((two[:edge] + three[edge : 2 * edge]) + small)

    def advance(state):
        x, r, p, rz = state
        q = times_system(p)
        pq = jnp.sum(p * q, axis=1, keepdims=True)
        alpha = jnp.where(pq > 0, rz / jnp.where(pq > 0, pq, 1.0), 0.0)
        x = x + alpha * p
        r = r - alpha * q
        z = r * inverse
        new_rz = jnp.sum(r * z, axis=1, keepdims=True)
        beta = jnp.where(rz > 0, new_rz / jnp.where(rz > 0, rz, 1.0), 0.0)
        return x, r, z + beta * p, new_rz

    def excess(r):
        return jnp.max(jnp.sum(r * r, axis=1, keepdims=True) - limit)

    z = goal * inverse
    state = (jnp.zeros_like(goal), goal, z, jnp.sum(goal * z, axis=1, keepdims=True))
    for _ in range(FIXED_STEPS):
        state = advance(state)

    def unfinished(carry):
        return (carry[0] < MOST_STEPS) & (carry[1] > 0)

    def more(carry):
        following = advance(carry[2])
        return carry[0] + 1, excess(following[1]), following

    _, left, state = lax.while_loop(unfinished, more, (0, excess(state[1]), state))
    out_ref[...] = state[0] * scale

    @pl.when(jnp.logical_not(left <= 0))
    def _():
        work[:rank] = system[...]
        work[rank:] = goal

        def sweep(column, carry):
            row = work[pl.ds(column, 1), :]
            pivot = jnp.sum(jnp.where(lanes == column, row, 0.0), axis=1, keepdims=True)
            current = work[...]
            factor = jnp.sum(jnp.where(lanes == column, current, 0.0), axis=1, keepdims=True) / pivot
            work[...] = jnp.where(lanes == column, factor, current - factor * row)
            return carry

        lax.fori_loop(0, rank, sweep, 0)
        out_ref[...] = work[rank:] * scale


def solve(shape, me, moment, gram_b, gram_c, edge):
    rank = moment.shape[-1]
    sources = shape[0] * shape[1]
    vmem = pl.BlockSpec(memory_space=pltpu.VMEM)
    return pl.pallas_call(
        functools.partial(solve_kernel, shape),
        out_shape=jax.ShapeDtypeStruct((edge, rank), jnp.float32),
        in_specs=[pl.BlockSpec(memory_space=pltpu.SMEM), vmem, vmem, vmem],
        out_specs=vmem,
        scratch_shapes=[
            pltpu.VMEM((rank, rank), jnp.float32),
            pltpu.VMEM((3, rank, rank), jnp.bfloat16),
            pltpu.VMEM((rank + edge, rank), jnp.float32),
            pltpu.SMEM((sources + 1,), jnp.int32),
            pltpu.SMEM((sources + 1,), jnp.int32),
        ],
        compiler_params=pltpu.CompilerParams(
            vmem_limit_bytes=(gram_b.size + gram_c.size) * 4 + 8 * MIB
        ),
        name="solve",
    )(me, moment, gram_b, gram_c)


def body(blocks, factor_b, factor_c, block_coords, block_count):
    edge = blocks.shape[1]
    rank = factor_b.shape[1]
    size_ja, size_ka = lax.axis_size("ja"), lax.axis_size("ka")
    devices = size_ja * size_ka
    second_dev = factor_b.shape[0] // edge
    third_dev = factor_c.shape[0] // edge
    assert devices & (devices - 1) == 0 and size_ja >= 2 and devices <= rank
    assert second_dev * third_dev < 256 and third_dev % 2 == 0
    plan = stage_plan(size_ja, size_ka)
    order = [bit for group in reversed(plan) for bit in group]
    index = lax.axis_index(ALL)
    core = lax.rem(lax.axis_index("ja"), 2)
    me = jnp.stack([index, core]).astype(jnp.int32)
    b_blocks = factor_b.reshape(second_dev, edge, rank)
    c_blocks = factor_c.reshape(third_dev, edge, rank)
    core_mask = size_ka

    b_parts, b_place, held = [b_blocks], [0] * size_ja, [0]
    for bit in list(range(1, size_ja.bit_length() - 1)) + [0]:
        b_parts = b_parts + [xor_permute(part, size_ka << bit) for part in b_parts]
        held = held + [q ^ (1 << bit) for q in held]
    for place, q in enumerate(held):
        b_place[q] = place
    c_half = lax.dynamic_slice_in_dim(c_blocks, core * (third_dev // 2), third_dev // 2, 0)
    c_place, held = [0] * size_ka, [0]
    for bit in [0] + list(reversed(range(1, size_ka.bit_length() - 1))):
        c_half = jnp.concatenate([c_half, xor_permute(c_half, 1 << bit)], axis=0)
        held = held + [q ^ (1 << bit) for q in held]
    for place, q in enumerate(held):
        c_place[q] = place
    c_other = xor_permute(c_half, core_mask)
    gram_b = grams_of(b_parts)
    gram_c = grams_of([c_half, c_other])

    keep, send = own_terms(order, blocks, b_blocks, c_blocks, block_coords, block_count, me, devices)
    received = xor_permute(send, core_mask)
    total = keep.astype(jnp.float32) + received.astype(jnp.float32)
    for group in plan[1:]:
        pieces = total.reshape((1 << len(group), -1) + total.shape[1:])
        total = pieces[0]
        arrived = []
        for piece in range(1, 1 << len(group)):
            mask = sum(1 << bit for i, bit in enumerate(group) if piece >> i & 1)
            arrived.append(xor_permute(pieces[piece].astype(jnp.bfloat16), mask))
        for part in arrived:
            total = total + part.astype(jnp.float32)
    shape = (size_ja, size_ka, second_dev, third_dev, tuple(b_place), tuple(c_place))
    return solve(shape, me, total[0], gram_b, gram_c, edge)


def solution(mesh):
    placed = (P(ALL, None, None), P("ja", None), P("ka", None), P(ALL, None), P(ALL))
    return jax.shard_map(body, mesh=mesh, in_specs=placed, out_specs=P(ALL, None), check_vma=False)
```

profile of v0, /device:TPU:0, one launch (start us, length us, event | category | flops | bytes accessed | tf_op | source)
XLA Modules:
  0.0 55.4 jit_solution(5127664116391570292)
XLA Ops:
  0.7 0.1 pad_add_fusion.me
  0.7 0.0 copy-start.1
  0.7 0.0 copy-start
  0.7 15.1 %own_terms.1 = (bf16[16,72,256]{2,1,0:T(8,128)(2,1)S(1)}, bf16[16,72,256]{2,1,0:T(8,128)(2,1)S(1)}) custom-call(s32[3,32]{1,0:T(4,128)} %bitcast.13, s32[1]{0:T(128)S(6)} %copy.6.count, s32[2]{0:T(128)S(1)} %pad_add_fusion.me, bf16[32,64,4096]{2,1,0:T(8,128)(2,1)} %blocks.1, bf16[8,64,256]{2,1,0:T(8,128)(2,1)} %bitcast.7, bf16[4,64,256]{2,1,0:T(8,128)(2,1)} %bitcast.11), custom_call_target="tpu_custom_call" | custom-call | flops 4294967296 | bytes 16777216 | tf_op jit(solution)/shard_map/own_terms/pallas_call | solution.py:169
  15.8 0.1 collective-permute-start
  15.9 0.0 copy-done.1
  15.9 0.4 collective-permute-start.10
  16.3 4.2 %collective-permute-done.10 = bf16[2,64,256]{2,1,0:T(8,128)(2,1)S(1)} collective-permute-done((bf16[2,64,256]{2,1,0:T(8,128)(2,1)S(1)}, bf16[2,64,256]{2,1,0:T(8,128)(2,1)S(1)}, u32[]{:S(2)}, u32[]{:S(2)}) %collective-permute-start.10) | collective-permute-done | bytes 65568 | tf_op jit(solution)/shard_map/ppermute | solution.py:23
  20.5 0.1 collective-permute-start.11
  20.5 0.0 copy-done
  20.6 1.3 %collective-permute-start.7 = (bf16[8,64,256]{2,1,0:T(8,128)(2,1)S(1)}, bf16[8,64,256]{2,1,0:T(8,128)(2,1)S(1)}, u32[]{:S(2)}, u32[]{:S(2)}) collective-permute-start(bf16[8,64,256]{2,1,0:T(8,128)(2,1)S(1)} %bitcast.8), channel_id=1, source_target_pairs={{0,16},{1,17},{2,18},{3,19},{4,20},{5,21},{6,22},{7,23},{8,24},{9,... | collective-permute-start | bytes 786440 | tf_op jit(solution)/shard_map/ppermute | solution.py:23
  21.8 7.5 %collective-permute-done.11 = bf16[4,64,256]{2,1,0:T(8,128)(2,1)S(1)} collective-permute-done((bf16[4,64,256]{2,1,0:T(8,128)(2,1)S(1)}, bf16[4,64,256]{2,1,0:T(8,128)(2,1)S(1)}, u32[]{:S(2)}, u32[]{:S(2)}) %collective-permute-start.11) | collective-permute-done | bytes 131104 | tf_op jit(solution)/shard_map/ppermute | solution.py:23
  29.3 0.1 collective-permute-start.12
  29.4 0.0 collective-permute-done
  29.4 0.2 convert_add_fusion
  29.6 0.9 %collective-permute-start.1 = (bf16[4,72,256]{2,1,0:T(8,128)(2,1)S(1)}, bf16[4,72,256]{2,1,0:T(8,128)(2,1)S(1)}, u32[]{:S(2)}, u32[]{:S(2)}) collective-permute-start(bf16[4,72,256]{2,1,0:T(8,128)(2,1)S(1)} %get-tuple-element.13), channel_id=1, source_target_pairs={{0,16},{1,17},{2,18},{3,19},{4,20},{5,21},{6,22},{7,23},{8,24},{9,... | collective-permute-start | bytes 442376 | tf_op jit(solution)/shard_map/ppermute | solution.py:23
  30.6 1.4 %collective-permute-start.3 = (bf16[4,72,256]{2,1,0:T(8,128)(2,1)S(1)}, bf16[4,72,256]{2,1,0:T(8,128)(2,1)S(1)}, u32[]{:S(2)}, u32[]{:S(2)}) collective-permute-start(bf16[4,72,256]{2,1,0:T(8,128)(2,1)S(1)} %get-tuple-element.14), channel_id=1, source_target_pairs={{0,17},{1,16},{2,19},{3,18},{4,21},{5,20},{6,23},{7,22},{8,25},{9,... | collective-permute-start | bytes 442376 | tf_op jit(solution)/shard_map/ppermute | solution.py:23
  31.9 1.2 %collective-permute-start.2 = (bf16[4,72,256]{2,1,0:T(8,128)(2,1)S(1)}, bf16[4,72,256]{2,1,0:T(8,128)(2,1)S(1)}, u32[]{:S(2)}, u32[]{:S(2)}) collective-permute-start(bf16[4,72,256]{2,1,0:T(8,128)(2,1)S(1)} %get-tuple-element.15), channel_id=1, source_target_pairs={{0,1},{1,0},{2,3},{3,2},{4,5},{5,4},{6,7},{7,6},{8,9},{9,8},{10,11... | collective-permute-start | bytes 442376 | tf_op jit(solution)/shard_map/ppermute | solution.py:23
  33.2 0.0 collective-permute-done.7.refs_1_
  33.2 0.0 collective-permute-start.8
  33.2 2.6 %collective-permute-done.12 = bf16[8,64,256]{2,1,0:T(8,128)(2,1)S(1)} collective-permute-done((bf16[8,64,256]{2,1,0:T(8,128)(2,1)S(1)}, bf16[8,64,256]{2,1,0:T(8,128)(2,1)S(1)}, u32[]{:S(2)}, u32[]{:S(2)}) %collective-permute-start.12) | collective-permute-done | bytes 262176 | tf_op jit(solution)/shard_map/ppermute | solution.py:23
  35.7 0.0 collective-permute-start.9
  35.8 0.1 pad_maximum_fusion.refs_0_
  35.8 0.4 collective-permute-done.1
  36.2 0.2 collective-permute-start.13
  36.4 1.9 %collective-permute-done.3 = bf16[4,72,256]{2,1,0:T(8,128)(2,1)S(1)} collective-permute-done((bf16[4,72,256]{2,1,0:T(8,128)(2,1)S(1)}, bf16[4,72,256]{2,1,0:T(8,128)(2,1)S(1)}, u32[]{:S(2)}, u32[]{:S(2)}) %collective-permute-start.3) | collective-permute-done | bytes 147488 | tf_op jit(solution)/shard_map/ppermute | solution.py:23
  38.3 1.1 %collective-permute-done.2 = bf16[4,72,256]{2,1,0:T(8,128)(2,1)S(1)} collective-permute-done((bf16[4,72,256]{2,1,0:T(8,128)(2,1)S(1)}, bf16[4,72,256]{2,1,0:T(8,128)(2,1)S(1)}, u32[]{:S(2)}, u32[]{:S(2)}) %collective-permute-start.2) | collective-permute-done | bytes 147488 | tf_op jit(solution)/shard_map/ppermute | solution.py:23
  39.4 0.1 fusion.6
  39.5 1.7 %collective-permute-start.4 = (bf16[1,72,256]{2,1,0:T(8,128)(2,1)S(1)}, bf16[1,72,256]{2,1,0:T(8,128)(2,1)S(1)}, u32[]{:S(2)}, u32[]{:S(2)}) collective-permute-start(bf16[1,72,256]{2,1,0:T(8,128)(2,1)S(1)} %get-tuple-element.16), channel_id=1, source_target_pairs={{0,2},{1,3},{2,0},{3,1},{4,6},{5,7},{6,4},{7,5},{8,10},{9,11},{10,... | collective-permute-start | bytes 110600 | tf_op jit(solution)/shard_map/ppermute | solution.py:23
  41.2 1.7 %collective-permute-start.6 = (bf16[1,72,256]{2,1,0:T(8,128)(2,1)S(1)}, bf16[1,72,256]{2,1,0:T(8,128)(2,1)S(1)}, u32[]{:S(2)}, u32[]{:S(2)}) collective-permute-start(bf16[1,72,256]{2,1,0:T(8,128)(2,1)S(1)} %get-tuple-element.17), channel_id=1, source_target_pairs={{0,6},{1,7},{2,4},{3,5},{4,2},{5,3},{6,0},{7,1},{8,14},{9,15},{10,... | collective-permute-start | bytes 110600 | tf_op jit(solution)/shard_map/ppermute | solution.py:23
  42.8 0.0 collective-permute-done.8.refs_2_
  42.8 0.2 collective-permute-start.5
  43.0 0.0 collective-permute-done.9.refs_3_
  43.0 1.3 %grams.2.gram_b = f32[32,256,256]{2,1,0:T(8,128)S(1)} custom-call(bf16[8,64,256]{2,1,0:T(8,128)(2,1)S(1)} %bitcast.10, bf16[8,64,256]{2,1,0:T(8,128)(2,1)S(1)} %collective-permute-done.7.refs_1_, bf16[8,64,256]{2,1,0:T(8,128)(2,1)S(1)} %collective-permute-done.8.refs_2_, bf16[8,64,256]{2,1,0:T(8,128)(2,1)S(1)} %collective-permute-done.9.refs_3_), custom_call_target="tpu_custom_call" | custom-call | flops 268435456 | bytes 1048576 | tf_op jit(solution)/shard_map/grams/pallas_call | solution.py:214
  44.3 0.0 collective-permute-done.4
  44.3 2.6 %collective-permute-done.6 = bf16[1,72,256]{2,1,0:T(8,128)(2,1)S(1)} collective-permute-done((bf16[1,72,256]{2,1,0:T(8,128)(2,1)S(1)}, bf16[1,72,256]{2,1,0:T(8,128)(2,1)S(1)}, u32[]{:S(2)}, u32[]{:S(2)}) %collective-permute-start.6) | collective-permute-done | bytes 36896 | tf_op jit(solution)/shard_map/ppermute | solution.py:23
  46.9 0.8 %collective-permute-done.5 = bf16[1,72,256]{2,1,0:T(8,128)(2,1)S(1)} collective-permute-done((bf16[1,72,256]{2,1,0:T(8,128)(2,1)S(1)}, bf16[1,72,256]{2,1,0:T(8,128)(2,1)S(1)}, u32[]{:S(2)}, u32[]{:S(2)}) %collective-permute-start.5) | collective-permute-done | bytes 36896 | tf_op jit(solution)/shard_map/ppermute | solution.py:23
  47.7 0.0 collective-permute-done.13.refs_1_
  47.8 1.3 %grams.3.gram_c = f32[32,256,256]{2,1,0:T(8,128)S(1)} custom-call(bf16[16,64,256]{2,1,0:T(8,128)(2,1)S(1)} %pad_maximum_fusion.refs_0_, bf16[16,64,256]{2,1,0:T(8,128)(2,1)S(1)} %collective-permute-done.13.refs_1_), custom_call_target="tpu_custom_call" | custom-call | flops 268435456 | bytes 1048576 | tf_op jit(solution)/shard_map/grams/pallas_call | solution.py:214
  49.1 6.4 %solve.1 = f32[64,256]{1,0:T(8,128)} custom-call(s32[2]{0:T(128)S(1)} %pad_add_fusion.me, f32[72,256]{1,0:T(8,128)S(1)} %fusion.4.moment_ref, f32[32,256,256]{2,1,0:T(8,128)S(1)} %grams.2.gram_b, f32[32,256,256]{2,1,0:T(8,128)S(1)} %grams.3.gram_c), custom_call_target="tpu_custom_call" | custom-call | tf_op jit(solution)/shard_map/solve/pallas_call | solution.py:344
  (6 shorter events, 0.1 us)
Async XLA Ops:
  0.7 15.2 %copy-start.1 = (bf16[256,256]{1,0:T(8,128)(2,1)S(1)}, bf16[256,256]{1,0:T(8,128)(2,1)}, u32[]{:S(2)}) copy-start(bf16[256,256]{1,0:T(8,128)(2,1)} %param.7) | copy-start | bytes 393220
  0.7 19.8 %copy-start = (bf16[512,256]{1,0:T(8,128)(2,1)S(1)}, bf16[512,256]{1,0:T(8,128)(2,1)}, u32[]{:S(2)}) copy-start(bf16[512,256]{1,0:T(8,128)(2,1)} %param.6) | copy-start | bytes 786436
  15.8 13.6 %collective-permute-start = (bf16[16,72,256]{2,1,0:T(8,128)(2,1)S(1)}, bf16[16,72,256]{2,1,0:T(8,128)(2,1)S(1)}, u32[]{:S(2)}, u32[]{:S(2)}) collective-permute-start(bf16[16,72,256]{2,1,0:T(8,128)(2,1)S(1)} %get-tuple-element.8), channel_id=1, source_target_pairs={{0,8},{1,9},{2,10},{3,11},{4,12},{5,13},{6,14},{7,15},{8,0},{9,1},... | collective-permute-start | bytes 1769480 | tf_op jit(solution)/shard_map/ppermute | solution.py:23
  15.9 4.5 %collective-permute-start.10 = (bf16[2,64,256]{2,1,0:T(8,128)(2,1)S(1)}, bf16[2,64,256]{2,1,0:T(8,128)(2,1)S(1)}, u32[]{:S(2)}, u32[]{:S(2)}) collective-permute-start(bf16[2,64,256]{2,1,0:T(8,128)(2,1)S(1)} %constant_dynamic-slice_fusion), channel_id=1, source_target_pairs={{0,1},{1,0},{2,3},{3,2},{4,5},{5,4},{6,7},{7,6},{8,9},{9,8},{10,11... | collective-permute-start | bytes 196616 | tf_op jit(solution)/shard_map/ppermute | solution.py:23
  20.5 8.8 %collective-permute-start.11 = (bf16[4,64,256]{2,1,0:T(8,128)(2,1)S(1)}, bf16[4,64,256]{2,1,0:T(8,128)(2,1)S(1)}, u32[]{:S(2)}, u32[]{:S(2)}) collective-permute-start(bf16[4,64,256]{2,1,0:T(8,128)(2,1)S(1)} %pad_maximum_fusion.2), channel_id=1, source_target_pairs={{0,4},{1,5},{2,6},{3,7},{4,0},{5,1},{6,2},{7,3},{8,12},{9,13},{10,... | collective-permute-start | bytes 393224 | tf_op jit(solution)/shard_map/ppermute | solution.py:23
  20.6 12.6 %collective-permute-start.7 = (bf16[8,64,256]{2,1,0:T(8,128)(2,1)S(1)}, bf16[8,64,256]{2,1,0:T(8,128)(2,1)S(1)}, u32[]{:S(2)}, u32[]{:S(2)}) collective-permute-start(bf16[8,64,256]{2,1,0:T(8,128)(2,1)S(1)} %bitcast.8), channel_id=1, source_target_pairs={{0,16},{1,17},{2,18},{3,19},{4,20},{5,21},{6,22},{7,23},{8,24},{9,... | collective-permute-start | bytes 786440 | tf_op jit(solution)/shard_map/ppermute | solution.py:23
  29.3 6.4 %collective-permute-start.12 = (bf16[8,64,256]{2,1,0:T(8,128)(2,1)S(1)}, bf16[8,64,256]{2,1,0:T(8,128)(2,1)S(1)}, u32[]{:S(2)}, u32[]{:S(2)}) collective-permute-start(bf16[8,64,256]{2,1,0:T(8,128)(2,1)S(1)} %pad_maximum_fusion.1), channel_id=1, source_target_pairs={{0,2},{1,3},{2,0},{3,1},{4,6},{5,7},{6,4},{7,5},{8,10},{9,11},{10,... | collective-permute-start | bytes 786440 | tf_op jit(solution)/shard_map/ppermute | solution.py:23
  29.6 6.6 %collective-permute-start.1 = (bf16[4,72,256]{2,1,0:T(8,128)(2,1)S(1)}, bf16[4,72,256]{2,1,0:T(8,128)(2,1)S(1)}, u32[]{:S(2)}, u32[]{:S(2)}) collective-permute-start(bf16[4,72,256]{2,1,0:T(8,128)(2,1)S(1)} %get-tuple-element.13), channel_id=1, source_target_pairs={{0,16},{1,17},{2,18},{3,19},{4,20},{5,21},{6,22},{7,23},{8,24},{9,... | collective-permute-start | bytes 442376 | tf_op jit(solution)/shard_map/ppermute | solution.py:23
  30.6 7.7 %collective-permute-start.3 = (bf16[4,72,256]{2,1,0:T(8,128)(2,1)S(1)}, bf16[4,72,256]{2,1,0:T(8,128)(2,1)S(1)}, u32[]{:S(2)}, u32[]{:S(2)}) collective-permute-start(bf16[4,72,256]{2,1,0:T(8,128)(2,1)S(1)} %get-tuple-element.14), channel_id=1, source_target_pairs={{0,17},{1,16},{2,19},{3,18},{4,21},{5,20},{6,23},{7,22},{8,25},{9,... | collective-permute-start | bytes 442376 | tf_op jit(solution)/shard_map/ppermute | solution.py:23
  31.9 7.5 %collective-permute-start.2 = (bf16[4,72,256]{2,1,0:T(8,128)(2,1)S(1)}, bf16[4,72,256]{2,1,0:T(8,128)(2,1)S(1)}, u32[]{:S(2)}, u32[]{:S(2)}) collective-permute-start(bf16[4,72,256]{2,1,0:T(8,128)(2,1)S(1)} %get-tuple-element.15), channel_id=1, source_target_pairs={{0,1},{1,0},{2,3},{3,2},{4,5},{5,4},{6,7},{7,6},{8,9},{9,8},{10,11... | collective-permute-start | bytes 442376 | tf_op jit(solution)/shard_map/ppermute | solution.py:23
  33.2 9.7 %collective-permute-start.8 = (bf16[8,64,256]{2,1,0:T(8,128)(2,1)S(1)}, bf16[8,64,256]{2,1,0:T(8,128)(2,1)S(1)}, u32[]{:S(2)}, u32[]{:S(2)}) collective-permute-start(bf16[8,64,256]{2,1,0:T(8,128)(2,1)S(1)} %bitcast.9), channel_id=1, source_target_pairs={{0,8},{1,9},{2,10},{3,11},{4,12},{5,13},{6,14},{7,15},{8,0},{9,1},... | collective-permute-start | bytes 786440 | tf_op jit(solution)/shard_map/ppermute | solution.py:23
  35.7 7.3 %collective-permute-start.9 = (bf16[8,64,256]{2,1,0:T(8,128)(2,1)S(1)}, bf16[8,64,256]{2,1,0:T(8,128)(2,1)S(1)}, u32[]{:S(2)}, u32[]{:S(2)}) collective-permute-start(bf16[8,64,256]{2,1,0:T(8,128)(2,1)S(1)} %collective-permute-done.7.refs_1_), channel_id=1, source_target_pairs={{0,8},{1,9},{2,10},{3,11},{4,12},{5,13},{6,14},{7,15},{8,0},{9,1},... | collective-permute-start | bytes 786440 | tf_op jit(solution)/shard_map/ppermute | solution.py:23
  36.2 11.6 %collective-permute-start.13 = (bf16[16,64,256]{2,1,0:T(8,128)(2,1)S(1)}, bf16[16,64,256]{2,1,0:T(8,128)(2,1)S(1)}, u32[]{:S(2)}, u32[]{:S(2)}) collective-permute-start(bf16[16,64,256]{2,1,0:T(8,128)(2,1)S(1)} %pad_maximum_fusion.refs_0_), channel_id=1, source_target_pairs={{0,8},{1,9},{2,10},{3,11},{4,12},{5,13},{6,14},{7,15},{8,0},{9,1},... | collective-permute-start | bytes 1572872 | tf_op jit(solution)/shard_map/ppermute | solution.py:23
  39.5 4.9 %collective-permute-start.4 = (bf16[1,72,256]{2,1,0:T(8,128)(2,1)S(1)}, bf16[1,72,256]{2,1,0:T(8,128)(2,1)S(1)}, u32[]{:S(2)}, u32[]{:S(2)}) collective-permute-start(bf16[1,72,256]{2,1,0:T(8,128)(2,1)S(1)} %get-tuple-element.16), channel_id=1, source_target_pairs={{0,2},{1,3},{2,0},{3,1},{4,6},{5,7},{6,4},{7,5},{8,10},{9,11},{10,... | collective-permute-start | bytes 110600 | tf_op jit(solution)/shard_map/ppermute | solution.py:23
  41.2 5.8 %collective-permute-start.6 = (bf16[1,72,256]{2,1,0:T(8,128)(2,1)S(1)}, bf16[1,72,256]{2,1,0:T(8,128)(2,1)S(1)}, u32[]{:S(2)}, u32[]{:S(2)}) collective-permute-start(bf16[1,72,256]{2,1,0:T(8,128)(2,1)S(1)} %get-tuple-element.17), channel_id=1, source_target_pairs={{0,6},{1,7},{2,4},{3,5},{4,2},{5,3},{6,0},{7,1},{8,14},{9,15},{10,... | collective-permute-start | bytes 110600 | tf_op jit(solution)/shard_map/ppermute | solution.py:23
  42.8 4.9 %collective-permute-start.5 = (bf16[1,72,256]{2,1,0:T(8,128)(2,1)S(1)}, bf16[1,72,256]{2,1,0:T(8,128)(2,1)S(1)}, u32[]{:S(2)}, u32[]{:S(2)}) collective-permute-start(bf16[1,72,256]{2,1,0:T(8,128)(2,1)S(1)} %get-tuple-element.18), channel_id=1, source_target_pairs={{0,4},{1,5},{2,6},{3,7},{4,0},{5,1},{6,2},{7,3},{8,12},{9,13},{10,... | collective-permute-start | bytes 110600 | tf_op jit(solution)/shard_map/ppermute | solution.py:23
where the time goes:
time: 55.6 us; the launch traced here: 55.4 us
  Pallas kernels  24 us (43%)
  waiting for transfers between devices  21 us (38%)
  starting transfers between devices  9.17 us (16%)
  between operations  0.8 us (1%)
    ppermute x14, waiting for transfers between devices, xor_permute(): return lax.ppermute(value, ALL, [(i, i ^ mask) for i in range(count)])  21 us
    pallas_call x1, Pallas kernels, own_terms(): pl.pallas_call(functools.partial(terms_kernel, order), out_shape=(half, h...  15.1 us
    ppermute x14, starting transfers between devices, xor_permute(): return lax.ppermute(value, ALL, [(i, i ^ mask) for i in range(count)])  9.17 us
    pallas_call x1, Pallas kernels, solve(): pl.pallas_call(functools.partial(solve_kernel, shape), out_shape=jax.Shap...  6.38 us
    pallas_call x2, Pallas kernels, grams_of(): pl.pallas_call(grams_kernel, out_shape=jax.ShapeDtypeStruct((number, rank...  2.59 us
  transfers between devices with their start and end apart: 14, of which 8 were waited for; matrix products, arithmetic and copies ran while one was open for 1% of the time, Pallas kernels for 2%

commit v1 on v0

--- a/solution.py
+++ b/solution.py
@@ -11,6 +11,7 @@
 CODE_ROWS = 8
 AHEAD = 4
 GROUP = 8
+STRIP = 128
 RIDGE = 0.1
 TOLERANCE = 1e-6
 FIXED_STEPS = 6
@@ -33,8 +34,7 @@
 def terms_kernel(
     order,
     coords_hbm,
-    count,
-    me,
+    count_hbm,
     blocks,
     b_hbm,
     c_hbm,
@@ -46,30 +46,35 @@
     sems,
     factor_sems,
     coords,
+    count,
     waiting,
     first,
     second,
 ):
     edge, rank = c_ref.shape[1:]
     third_dev = c_ref.shape[0]
+    low_bits = (third_dev - 1).bit_length()
     half = keep_ref.shape[0]
-    live = count[0]
-    device = me[0]
+    device = lax.axis_index(ALL)
 
     def fetch(slot):
         return pltpu.make_async_copy(blocks.at[slot], held.at[slot], sems.at[slot])
 
-    factors = [
+    copies = [
         pltpu.make_async_copy(source, place, factor_sems.at[index])
-        for index, (source, place) in enumerate(((coords_hbm, coords), (b_hbm, b_ref), (c_hbm, c_ref)))
+        for index, (source, place) in enumerate(
+            ((coords_hbm, coords), (count_hbm, count), (b_hbm, b_ref), (c_hbm, c_ref))
+        )
     ]
-    for copy in factors:
+    for copy in copies:
         copy.start()
     fetch(0).start()
 
     for cell in range(waiting.shape[0]):
         waiting[cell] = -1
-    factors[0].wait()
+    copies[0].wait()
+    copies[1].wait()
+    live = count[0]
 
     def assign(slot, passes):
         cell = coords[1, slot] * third_dev + coords[2, slot]
@@ -102,7 +107,7 @@
 
     keep_ref[...] = jnp.zeros_like(keep_ref)
     send_ref[...] = jnp.zeros_like(send_ref)
-    for copy in factors[1:]:
+    for copy in copies[2:]:
         copy.wait()
     lanes = lax.broadcasted_iota(jnp.int32, (CODE_ROWS, rank), 1)
 
@@ -150,7 +155,7 @@
             part = jnp.concatenate([held[one, :, columns], held[two, :, columns]], axis=0)
             total += jnp.dot(part, khatri, preferred_element_type=jnp.float32)
         term = total.astype(jnp.bfloat16)
-        code = (b_index * third_dev + c_index + 1).astype(jnp.float32)
+        code = ((b_index << low_bits | c_index) << 1 | 1).astype(jnp.float32)
         put(one, code, term[:edge])
         put(two, code, term[edge:])
         return carry
@@ -158,26 +163,26 @@
     lax.fori_loop(0, passes, step, 0)
 
 
-def own_terms(order, blocks, b_blocks, c_blocks, coords, count, me, total_rows):
+def own_terms(order, blocks, b_blocks, c_blocks, coords, count, total_rows):
     slots, edge, width = blocks.shape
     rank = b_blocks.shape[2]
     half = jax.ShapeDtypeStruct((total_rows // 2, edge + CODE_ROWS, rank), jnp.bfloat16)
-    smem = pl.BlockSpec(memory_space=pltpu.SMEM)
     vmem = pl.BlockSpec(memory_space=pltpu.VMEM)
     hbm = pl.BlockSpec(memory_space=pltpu.HBM)
     in_hbm = functools.partial(pltpu.with_memory_space_constraint, memory_space=pltpu.HBM)
     return pl.pallas_call(
         functools.partial(terms_kernel, order),
         out_shape=(half, half),
-        in_specs=[hbm, smem, smem, hbm, hbm, hbm],
+        in_specs=[hbm, pl.BlockSpec(memory_space=pl.ANY), hbm, hbm, hbm],
         out_specs=(vmem, vmem),
         scratch_shapes=[
             pltpu.VMEM((slots, edge, width), blocks.dtype),
             pltpu.VMEM(b_blocks.shape, b_blocks.dtype),
             pltpu.VMEM(c_blocks.shape, c_blocks.dtype),
             pltpu.SemaphoreType.DMA((slots,)),
-            pltpu.SemaphoreType.DMA((3,)),
+            pltpu.SemaphoreType.DMA((4,)),
             pltpu.SMEM((3, slots), jnp.int32),
+            pltpu.SMEM((1,), jnp.int32),
             pltpu.SMEM((b_blocks.shape[0] * c_blocks.shape[0],), jnp.int32),
             pltpu.SMEM((slots,), jnp.int32),
             pltpu.SMEM((slots,), jnp.int32),
@@ -189,7 +194,7 @@
             transcendentals=0,
         ),
         name="own_terms",
-    )(in_hbm(coords.T), count, me, blocks, in_hbm(b_blocks), in_hbm(c_blocks))
+    )(in_hbm(coords.T), count, *(in_hbm(operand) for operand in (blocks, b_blocks, c_blocks)))
 
 
 def grams_kernel(*refs):
@@ -233,14 +238,15 @@
     return high, middle, (rest - middle.astype(jnp.float32)).astype(jnp.bfloat16)
 
 
-def solve_kernel(shape, me, moment_ref, gram_b, gram_c, out_ref, system, parts, work, b_list, c_list):
+def solve_kernel(shape, moment_ref, gram_b, gram_c, out_ref, system, parts, work, b_list, c_list):
     size_ja, size_ka, second_dev, third_dev, b_place, c_place = shape
     edge, rank = out_ref.shape
     sources = size_ja * size_ka
     lanes = lax.broadcasted_iota(jnp.int32, (1, rank), 1)
-    core = me[1]
-
-    width = (second_dev * third_dev).bit_length()
+    core = lax.axis_index("ja") & 1
+
+    low_bits = (third_dev - 1).bit_length()
+    width = low_bits + (second_dev - 1).bit_length() + 1
     per = 24 // width
     weight = jnp.left_shift(1, width * lax.rem(lanes, per)).astype(jnp.float32)
     weighted = moment_ref[edge : edge + 1, :] * weight
@@ -252,14 +258,15 @@
     live = 0
     for source in range(sources):
         code = lax.shift_right_logical(packed[source // per], width * (source % per)) & ((1 << width) - 1)
-        cell = jnp.maximum(code - 1, 0)
-        second, third = lax.div(cell, third_dev), lax.rem(cell, third_dev)
-        far = jnp.bitwise_xor(lax.div(third, half), core)
+        field = lax.shift_right_logical(code, 1)
+        second, third = lax.shift_right_logical(field, low_bits), field & ((1 << low_bits) - 1)
+        upper = (third >= half).astype(jnp.int32)
+        far = jnp.bitwise_xor(upper, core)
         b_list[live] = b_place[source // size_ka] * second_dev + second
-        c_list[live] = (far * size_ka + c_place[source % size_ka]) * half + lax.rem(third, half)
-        live = live + (code > 0).astype(jnp.int32)
-
-    strip = min(64, rank)
+        c_list[live] = (far * size_ka + c_place[source % size_ka]) * half + third - upper * half
+        live = live + (code & 1)
+
+    strip = min(STRIP, rank)
     for low in range(0, rank, strip):
         rows = lax.broadcasted_iota(jnp.int32, (strip, rank), 0) + low
         columns = lax.broadcasted_iota(jnp.int32, (strip, rank), 1)
@@ -337,14 +344,14 @@
         out_ref[...] = work[rank:] * scale
 
 
-def solve(shape, me, moment, gram_b, gram_c, edge):
+def solve(shape, moment, gram_b, gram_c, edge):
     rank = moment.shape[-1]
     sources = shape[0] * shape[1]
     vmem = pl.BlockSpec(memory_space=pltpu.VMEM)
     return pl.pallas_call(
         functools.partial(solve_kernel, shape),
         out_shape=jax.ShapeDtypeStruct((edge, rank), jnp.float32),
-        in_specs=[pl.BlockSpec(memory_space=pltpu.SMEM), vmem, vmem, vmem],
+        in_specs=[vmem, vmem, vmem],
         out_specs=vmem,
         scratch_shapes=[
             pltpu.VMEM((rank, rank), jnp.float32),
@@ -357,7 +364,7 @@
             vmem_limit_bytes=(gram_b.size + gram_c.size) * 4 + 8 * MIB
         ),
         name="solve",
-    )(me, moment, gram_b, gram_c)
+    )(moment, gram_b, gram_c)
 
 
 def body(blocks, factor_b, factor_c, block_coords, block_count):
@@ -368,12 +375,10 @@
     second_dev = factor_b.shape[0] // edge
     third_dev = factor_c.shape[0] // edge
     assert devices & (devices - 1) == 0 and size_ja >= 2 and devices <= rank
-    assert second_dev * third_dev < 256 and third_dev % 2 == 0
+    assert second_dev * third_dev <= 64 and third_dev % 2 == 0
     plan = stage_plan(size_ja, size_ka)
     order = [bit for group in reversed(plan) for bit in group]
-    index = lax.axis_index(ALL)
-    core = lax.rem(lax.axis_index("ja"), 2)
-    me = jnp.stack([index, core]).astype(jnp.int32)
+    core = lax.axis_index("ja") & 1
     b_blocks = factor_b.reshape(second_dev, edge, rank)
     c_blocks = factor_c.reshape(third_dev, edge, rank)
     core_mask = size_ka
@@ -386,16 +391,21 @@
         b_place[q] = place
     c_half = lax.dynamic_slice_in_dim(c_blocks, core * (third_dev // 2), third_dev // 2, 0)
     c_place, held = [0] * size_ka, [0]
-    for bit in [0] + list(reversed(range(1, size_ka.bit_length() - 1))):
-        c_half = jnp.concatenate([c_half, xor_permute(c_half, 1 << bit)], axis=0)
-        held = held + [q ^ (1 << bit) for q in held]
+    top = size_ka.bit_length() - 2
+    for group in [[0]] + [[bit] for bit in range(top, 0, -1)]:
+        masks = [sum(1 << bit for i, bit in enumerate(group) if piece >> i & 1) for piece in range(1 << len(group))]
+        arrived = [c_half]
+        for piece, mask in enumerate(masks[1:], 1):
+            arrived.append(xor_permute(c_half, mask))
+        c_half = jnp.concatenate(arrived, axis=0)
+        held = [q ^ mask for mask in masks for q in held]
     for place, q in enumerate(held):
         c_place[q] = place
     c_other = xor_permute(c_half, core_mask)
     gram_b = grams_of(b_parts)
     gram_c = grams_of([c_half, c_other])
 
-    keep, send = own_terms(order, blocks, b_blocks, c_blocks, block_coords, block_count, me, devices)
+    keep, send = own_terms(order, blocks, b_blocks, c_blocks, block_coords, block_count, devices)
     received = xor_permute(send, core_mask)
     total = keep.astype(jnp.float32) + received.astype(jnp.float32)
     for group in plan[1:]:
@@ -408,7 +418,7 @@
         for part in arrived:
             total = total + part.astype(jnp.float32)
     shape = (size_ja, size_ka, second_dev, third_dev, tuple(b_place), tuple(c_place))
-    return solve(shape, me, total[0], gram_b, gram_c, edge)
+    return solve(shape, total[0], gram_b, gram_c, edge)
 
 
 def solution(mesh):

time: 55.6 us -> 54.4 us (0.978)
  Pallas kernels: 24 us -> 22.9 us
    pallas_call x1, Pallas kernels: 6.38 us -> 5.66 us  [solve(): pl.pallas_call(functools.partial(solve_kernel, shape), out_shape=jax.Shap...]
where the time goes in v1:
time: 54.4 us; the launch traced here: 54.2 us
  Pallas kernels  22.9 us (42%)
  waiting for transfers between devices  20.9 us (38%)
  starting transfers between devices  9.17 us (17%)
  between operations  0.82 us (2%)
    ppermute x14, waiting for transfers between devices, xor_permute(): return lax.ppermute(value, ALL, [(i, i ^ mask) for i in range(count)])  20.9 us
    pallas_call x1, Pallas kernels, own_terms(): pl.pallas_call(functools.partial(terms_kernel, order), out_shape=(half, h...  14.7 us
    ppermute x14, starting transfers between devices, xor_permute(): return lax.ppermute(value, ALL, [(i, i ^ mask) for i in range(count)])  9.17 us
    pallas_call x1, Pallas kernels, solve(): pl.pallas_call(functools.partial(solve_kernel, shape), out_shape=jax.Shap...  5.66 us
    pallas_call x2, Pallas kernels, grams_of(): pl.pallas_call(grams_kernel, out_shape=jax.ShapeDtypeStruct((number, rank...  2.59 us
  transfers between devices with their start and end apart: 14, of which 8 were waited for; matrix products, arithmetic and copies ran while one was open for 1% of the time, Pallas kernels for 2%

profile of v1, /device:TPU:0, one launch (start us, length us, event | category | flops | bytes accessed | tf_op | source)
XLA Modules:
  0.0 54.2 jit_solution(13125293988378883076)
XLA Ops:
  0.7 0.0 copy-start.1
  0.7 0.0 copy-start
  0.7 14.7 %own_terms.1 = (bf16[16,72,256]{2,1,0:T(8,128)(2,1)S(1)}, bf16[16,72,256]{2,1,0:T(8,128)(2,1)S(1)}) custom-call(s32[3,32]{1,0:T(4,128)} %bitcast.11, s32[1]{0:T(128)S(6)} %copy.6.count_hbm, bf16[32,64,4096]{2,1,0:T(8,128)(2,1)} %blocks.1, bf16[8,64,256]{2,1,0:T(8,128)(2,1)} %bitcast.5, bf16[4,64,256]{2,1,0:T(8,128)(2,1)} %bitcast.9), custom_call_target="tpu_custom_call" | custom-call | flops 4294967296 | bytes 16777216 | tf_op jit(solution)/shard_map/own_terms/pallas_call | solution.py:173
  15.4 0.1 collective-permute-start
  15.5 0.0 copy-done.1
  15.5 0.3 collective-permute-start.10
  15.8 4.2 %collective-permute-done.10 = bf16[2,64,256]{2,1,0:T(8,128)(2,1)S(1)} collective-permute-done((bf16[2,64,256]{2,1,0:T(8,128)(2,1)S(1)}, bf16[2,64,256]{2,1,0:T(8,128)(2,1)S(1)}, u32[]{:S(2)}, u32[]{:S(2)}) %collective-permute-start.10) | collective-permute-done | bytes 65568 | tf_op jit(solution)/shard_map/ppermute | solution.py:24
  20.0 0.1 collective-permute-start.11
  20.1 0.0 copy-done
  20.1 1.2 %collective-permute-start.7 = (bf16[8,64,256]{2,1,0:T(8,128)(2,1)S(1)}, bf16[8,64,256]{2,1,0:T(8,128)(2,1)S(1)}, u32[]{:S(2)}, u32[]{:S(2)}) collective-permute-start(bf16[8,64,256]{2,1,0:T(8,128)(2,1)S(1)} %bitcast.6), channel_id=1, source_target_pairs={{0,16},{1,17},{2,18},{3,19},{4,20},{5,21},{6,22},{7,23},{8,24},{9,... | collective-permute-start | bytes 786440 | tf_op jit(solution)/shard_map/ppermute | solution.py:24
  21.3 7.5 %collective-permute-done.11 = bf16[4,64,256]{2,1,0:T(8,128)(2,1)S(1)} collective-permute-done((bf16[4,64,256]{2,1,0:T(8,128)(2,1)S(1)}, bf16[4,64,256]{2,1,0:T(8,128)(2,1)S(1)}, u32[]{:S(2)}, u32[]{:S(2)}) %collective-permute-start.11) | collective-permute-done | bytes 131104 | tf_op jit(solution)/shard_map/ppermute | solution.py:24
  28.9 0.1 collective-permute-start.12
  29.0 0.0 collective-permute-done
  29.0 0.1 convert_add_fusion
  29.2 0.9 %collective-permute-start.1 = (bf16[4,72,256]{2,1,0:T(8,128)(2,1)S(1)}, bf16[4,72,256]{2,1,0:T(8,128)(2,1)S(1)}, u32[]{:S(2)}, u32[]{:S(2)}) collective-permute-start(bf16[4,72,256]{2,1,0:T(8,128)(2,1)S(1)} %get-tuple-element.13), channel_id=1, source_target_pairs={{0,16},{1,17},{2,18},{3,19},{4,20},{5,21},{6,22},{7,23},{8,24},{9,... | collective-permute-start | bytes 442376 | tf_op jit(solution)/shard_map/ppermute | solution.py:24
  30.1 1.4 %collective-permute-start.3 = (bf16[4,72,256]{2,1,0:T(8,128)(2,1)S(1)}, bf16[4,72,256]{2,1,0:T(8,128)(2,1)S(1)}, u32[]{:S(2)}, u32[]{:S(2)}) collective-permute-start(bf16[4,72,256]{2,1,0:T(8,128)(2,1)S(1)} %get-tuple-element.14), channel_id=1, source_target_pairs={{0,17},{1,16},{2,19},{3,18},{4,21},{5,20},{6,23},{7,22},{8,25},{9,... | collective-permute-start | bytes 442376 | tf_op jit(solution)/shard_map/ppermute | solution.py:24
  31.5 1.2 %collective-permute-start.2 = (bf16[4,72,256]{2,1,0:T(8,128)(2,1)S(1)}, bf16[4,72,256]{2,1,0:T(8,128)(2,1)S(1)}, u32[]{:S(2)}, u32[]{:S(2)}) collective-permute-start(bf16[4,72,256]{2,1,0:T(8,128)(2,1)S(1)} %get-tuple-element.15), channel_id=1, source_target_pairs={{0,1},{1,0},{2,3},{3,2},{4,5},{5,4},{6,7},{7,6},{8,9},{9,8},{10,11... | collective-permute-start | bytes 442376 | tf_op jit(solution)/shard_map/ppermute | solution.py:24
  32.7 0.0 collective-permute-done.7.refs_1_
  32.7 0.0 collective-permute-start.8
  32.7 2.6 %collective-permute-done.12 = bf16[8,64,256]{2,1,0:T(8,128)(2,1)S(1)} collective-permute-done((bf16[8,64,256]{2,1,0:T(8,128)(2,1)S(1)}, bf16[8,64,256]{2,1,0:T(8,128)(2,1)S(1)}, u32[]{:S(2)}, u32[]{:S(2)}) %collective-permute-start.12) | collective-permute-done | bytes 262176 | tf_op jit(solution)/shard_map/ppermute | solution.py:24
  35.3 0.0 collective-permute-start.9
  35.3 0.1 pad_maximum_fusion.refs_0_
  35.4 0.3 collective-permute-done.1
  35.7 0.3 collective-permute-start.13
  36.0 1.9 %collective-permute-done.3 = bf16[4,72,256]{2,1,0:T(8,128)(2,1)S(1)} collective-permute-done((bf16[4,72,256]{2,1,0:T(8,128)(2,1)S(1)}, bf16[4,72,256]{2,1,0:T(8,128)(2,1)S(1)}, u32[]{:S(2)}, u32[]{:S(2)}) %collective-permute-start.3) | collective-permute-done | bytes 147488 | tf_op jit(solution)/shard_map/ppermute | solution.py:24
  37.9 1.1 %collective-permute-done.2 = bf16[4,72,256]{2,1,0:T(8,128)(2,1)S(1)} collective-permute-done((bf16[4,72,256]{2,1,0:T(8,128)(2,1)S(1)}, bf16[4,72,256]{2,1,0:T(8,128)(2,1)S(1)}, u32[]{:S(2)}, u32[]{:S(2)}) %collective-permute-start.2) | collective-permute-done | bytes 147488 | tf_op jit(solution)/shard_map/ppermute | solution.py:24
  38.9 0.1 fusion.6
  39.0 1.7 %collective-permute-start.4 = (bf16[1,72,256]{2,1,0:T(8,128)(2,1)S(1)}, bf16[1,72,256]{2,1,0:T(8,128)(2,1)S(1)}, u32[]{:S(2)}, u32[]{:S(2)}) collective-permute-start(bf16[1,72,256]{2,1,0:T(8,128)(2,1)S(1)} %get-tuple-element.16), channel_id=1, source_target_pairs={{0,2},{1,3},{2,0},{3,1},{4,6},{5,7},{6,4},{7,5},{8,10},{9,11},{10,... | collective-permute-start | bytes 110600 | tf_op jit(solution)/shard_map/ppermute | solution.py:24
  40.7 1.7 %collective-permute-start.6 = (bf16[1,72,256]{2,1,0:T(8,128)(2,1)S(1)}, bf16[1,72,256]{2,1,0:T(8,128)(2,1)S(1)}, u32[]{:S(2)}, u32[]{:S(2)}) collective-permute-start(bf16[1,72,256]{2,1,0:T(8,128)(2,1)S(1)} %get-tuple-element.17), channel_id=1, source_target_pairs={{0,6},{1,7},{2,4},{3,5},{4,2},{5,3},{6,0},{7,1},{8,14},{9,15},{10,... | collective-permute-start | bytes 110600 | tf_op jit(solution)/shard_map/ppermute | solution.py:24
  42.4 0.0 collective-permute-done.8.refs_2_
  42.4 0.2 collective-permute-start.5
  42.6 0.0 collective-permute-done.9.refs_3_
  42.6 1.3 %grams.2.gram_b = f32[32,256,256]{2,1,0:T(8,128)S(1)} custom-call(bf16[8,64,256]{2,1,0:T(8,128)(2,1)S(1)} %bitcast.8, bf16[8,64,256]{2,1,0:T(8,128)(2,1)S(1)} %collective-permute-done.7.refs_1_, bf16[8,64,256]{2,1,0:T(8,128)(2,1)S(1)} %collective-permute-done.8.refs_2_, bf16[8,64,256]{2,1,0:T(8,128)(2,1)S(1)} %collective-permute-done.9.refs_3_), custom_call_target="tpu_custom_call" | custom-call | flops 268435456 | bytes 1048576 | tf_op jit(solution)/shard_map/grams/pallas_call | solution.py:219
  43.9 0.0 collective-permute-done.4
  43.9 2.6 %collective-permute-done.6 = bf16[1,72,256]{2,1,0:T(8,128)(2,1)S(1)} collective-permute-done((bf16[1,72,256]{2,1,0:T(8,128)(2,1)S(1)}, bf16[1,72,256]{2,1,0:T(8,128)(2,1)S(1)}, u32[]{:S(2)}, u32[]{:S(2)}) %collective-permute-start.6) | collective-permute-done | bytes 36896 | tf_op jit(solution)/shard_map/ppermute | solution.py:24
  46.5 0.8 %collective-permute-done.5 = bf16[1,72,256]{2,1,0:T(8,128)(2,1)S(1)} collective-permute-done((bf16[1,72,256]{2,1,0:T(8,128)(2,1)S(1)}, bf16[1,72,256]{2,1,0:T(8,128)(2,1)S(1)}, u32[]{:S(2)}, u32[]{:S(2)}) %collective-permute-start.5) | collective-permute-done | bytes 36896 | tf_op jit(solution)/shard_map/ppermute | solution.py:24
  47.3 0.0 collective-permute-done.13.refs_1_
  47.3 1.3 %grams.3.gram_c = f32[32,256,256]{2,1,0:T(8,128)S(1)} custom-call(bf16[16,64,256]{2,1,0:T(8,128)(2,1)S(1)} %pad_maximum_fusion.refs_0_, bf16[16,64,256]{2,1,0:T(8,128)(2,1)S(1)} %collective-permute-done.13.refs_1_), custom_call_target="tpu_custom_call" | custom-call | flops 268435456 | bytes 1048576 | tf_op jit(solution)/shard_map/grams/pallas_call | solution.py:219
  48.6 5.7 %solve.1 = f32[64,256]{1,0:T(8,128)} custom-call(f32[72,256]{1,0:T(8,128)S(1)} %fusion.4.moment_ref, f32[32,256,256]{2,1,0:T(8,128)S(1)} %grams.2.gram_b, f32[32,256,256]{2,1,0:T(8,128)S(1)} %grams.3.gram_c), custom_call_target="tpu_custom_call" | custom-call | tf_op jit(solution)/shard_map/solve/pallas_call | solution.py:351
  (6 shorter events, 0.1 us)
Async XLA Ops:
  0.7 14.8 %copy-start.1 = (bf16[256,256]{1,0:T(8,128)(2,1)S(1)}, bf16[256,256]{1,0:T(8,128)(2,1)}, u32[]{:S(2)}) copy-start(bf16[256,256]{1,0:T(8,128)(2,1)} %param.7) | copy-start | bytes 393220
  0.7 19.5 %copy-start = (bf16[512,256]{1,0:T(8,128)(2,1)S(1)}, bf16[512,256]{1,0:T(8,128)(2,1)}, u32[]{:S(2)}) copy-start(bf16[512,256]{1,0:T(8,128)(2,1)} %param.6) | copy-start | bytes 786436
  15.4 13.6 %collective-permute-start = (bf16[16,72,256]{2,1,0:T(8,128)(2,1)S(1)}, bf16[16,72,256]{2,1,0:T(8,128)(2,1)S(1)}, u32[]{:S(2)}, u32[]{:S(2)}) collective-permute-start(bf16[16,72,256]{2,1,0:T(8,128)(2,1)S(1)} %get-tuple-element.8), channel_id=1, source_target_pairs={{0,8},{1,9},{2,10},{3,11},{4,12},{5,13},{6,14},{7,15},{8,0},{9,1},... | collective-permute-start | bytes 1769480 | tf_op jit(solution)/shard_map/ppermute | solution.py:24
  15.5 4.5 %collective-permute-start.10 = (bf16[2,64,256]{2,1,0:T(8,128)(2,1)S(1)}, bf16[2,64,256]{2,1,0:T(8,128)(2,1)S(1)}, u32[]{:S(2)}, u32[]{:S(2)}) collective-permute-start(bf16[2,64,256]{2,1,0:T(8,128)(2,1)S(1)} %constant_dynamic-slice_fusion), channel_id=1, source_target_pairs={{0,1},{1,0},{2,3},{3,2},{4,5},{5,4},{6,7},{7,6},{8,9},{9,8},{10,11... | collective-permute-start | bytes 196616 | tf_op jit(solution)/shard_map/ppermute | solution.py:24
  20.0 8.8 %collective-permute-start.11 = (bf16[4,64,256]{2,1,0:T(8,128)(2,1)S(1)}, bf16[4,64,256]{2,1,0:T(8,128)(2,1)S(1)}, u32[]{:S(2)}, u32[]{:S(2)}) collective-permute-start(bf16[4,64,256]{2,1,0:T(8,128)(2,1)S(1)} %pad_maximum_fusion.2), channel_id=1, source_target_pairs={{0,4},{1,5},{2,6},{3,7},{4,0},{5,1},{6,2},{7,3},{8,12},{9,13},{10,... | collective-permute-start | bytes 393224 | tf_op jit(solution)/shard_map/ppermute | solution.py:24
  20.1 12.6 %collective-permute-start.7 = (bf16[8,64,256]{2,1,0:T(8,128)(2,1)S(1)}, bf16[8,64,256]{2,1,0:T(8,128)(2,1)S(1)}, u32[]{:S(2)}, u32[]{:S(2)}) collective-permute-start(bf16[8,64,256]{2,1,0:T(8,128)(2,1)S(1)} %bitcast.6), channel_id=1, source_target_pairs={{0,16},{1,17},{2,18},{3,19},{4,20},{5,21},{6,22},{7,23},{8,24},{9,... | collective-permute-start | bytes 786440 | tf_op jit(solution)/shard_map/ppermute | solution.py:24
  28.9 6.4 %collective-permute-start.12 = (bf16[8,64,256]{2,1,0:T(8,128)(2,1)S(1)}, bf16[8,64,256]{2,1,0:T(8,128)(2,1)S(1)}, u32[]{:S(2)}, u32[]{:S(2)}) collective-permute-start(bf16[8,64,256]{2,1,0:T(8,128)(2,1)S(1)} %pad_maximum_fusion.1), channel_id=1, source_target_pairs={{0,2},{1,3},{2,0},{3,1},{4,6},{5,7},{6,4},{7,5},{8,10},{9,11},{10,... | collective-permute-start | bytes 786440 | tf_op jit(solution)/shard_map/ppermute | solution.py:24
  29.2 6.5 %collective-permute-start.1 = (bf16[4,72,256]{2,1,0:T(8,128)(2,1)S(1)}, bf16[4,72,256]{2,1,0:T(8,128)(2,1)S(1)}, u32[]{:S(2)}, u32[]{:S(2)}) collective-permute-start(bf16[4,72,256]{2,1,0:T(8,128)(2,1)S(1)} %get-tuple-element.13), channel_id=1, source_target_pairs={{0,16},{1,17},{2,18},{3,19},{4,20},{5,21},{6,22},{7,23},{8,24},{9,... | collective-permute-start | bytes 442376 | tf_op jit(solution)/shard_map/ppermute | solution.py:24
  30.1 7.8 %collective-permute-start.3 = (bf16[4,72,256]{2,1,0:T(8,128)(2,1)S(1)}, bf16[4,72,256]{2,1,0:T(8,128)(2,1)S(1)}, u32[]{:S(2)}, u32[]{:S(2)}) collective-permute-start(bf16[4,72,256]{2,1,0:T(8,128)(2,1)S(1)} %get-tuple-element.14), channel_id=1, source_target_pairs={{0,17},{1,16},{2,19},{3,18},{4,21},{5,20},{6,23},{7,22},{8,25},{9,... | collective-permute-start | bytes 442376 | tf_op jit(solution)/shard_map/ppermute | solution.py:24
  31.5 7.4 %collective-permute-start.2 = (bf16[4,72,256]{2,1,0:T(8,128)(2,1)S(1)}, bf16[4,72,256]{2,1,0:T(8,128)(2,1)S(1)}, u32[]{:S(2)}, u32[]{:S(2)}) collective-permute-start(bf16[4,72,256]{2,1,0:T(8,128)(2,1)S(1)} %get-tuple-element.15), channel_id=1, source_target_pairs={{0,1},{1,0},{2,3},{3,2},{4,5},{5,4},{6,7},{7,6},{8,9},{9,8},{10,11... | collective-permute-start | bytes 442376 | tf_op jit(solution)/shard_map/ppermute | solution.py:24
  32.7 9.7 %collective-permute-start.8 = (bf16[8,64,256]{2,1,0:T(8,128)(2,1)S(1)}, bf16[8,64,256]{2,1,0:T(8,128)(2,1)S(1)}, u32[]{:S(2)}, u32[]{:S(2)}) collective-permute-start(bf16[8,64,256]{2,1,0:T(8,128)(2,1)S(1)} %bitcast.7), channel_id=1, source_target_pairs={{0,8},{1,9},{2,10},{3,11},{4,12},{5,13},{6,14},{7,15},{8,0},{9,1},... | collective-permute-start | bytes 786440 | tf_op jit(solution)/shard_map/ppermute | solution.py:24
  35.3 7.2 %collective-permute-start.9 = (bf16[8,64,256]{2,1,0:T(8,128)(2,1)S(1)}, bf16[8,64,256]{2,1,0:T(8,128)(2,1)S(1)}, u32[]{:S(2)}, u32[]{:S(2)}) collective-permute-start(bf16[8,64,256]{2,1,0:T(8,128)(2,1)S(1)} %collective-permute-done.7.refs_1_), channel_id=1, source_target_pairs={{0,8},{1,9},{2,10},{3,11},{4,12},{5,13},{6,14},{7,15},{8,0},{9,1},... | collective-permute-start | bytes 786440 | tf_op jit(solution)/shard_map/ppermute | solution.py:24
  35.7 11.6 %collective-permute-start.13 = (bf16[16,64,256]{2,1,0:T(8,128)(2,1)S(1)}, bf16[16,64,256]{2,1,0:T(8,128)(2,1)S(1)}, u32[]{:S(2)}, u32[]{:S(2)}) collective-permute-start(bf16[16,64,256]{2,1,0:T(8,128)(2,1)S(1)} %pad_maximum_fusion.refs_0_), channel_id=1, source_target_pairs={{0,8},{1,9},{2,10},{3,11},{4,12},{5,13},{6,14},{7,15},{8,0},{9,1},... | collective-permute-start | bytes 1572872 | tf_op jit(solution)/shard_map/ppermute | solution.py:24
  39.0 4.9 %collective-permute-start.4 = (bf16[1,72,256]{2,1,0:T(8,128)(2,1)S(1)}, bf16[1,72,256]{2,1,0:T(8,128)(2,1)S(1)}, u32[]{:S(2)}, u32[]{:S(2)}) collective-permute-start(bf16[1,72,256]{2,1,0:T(8,128)(2,1)S(1)} %get-tuple-element.16), channel_id=1, source_target_pairs={{0,2},{1,3},{2,0},{3,1},{4,6},{5,7},{6,4},{7,5},{8,10},{9,11},{10,... | collective-permute-start | bytes 110600 | tf_op jit(solution)/shard_map/ppermute | solution.py:24
  40.7 5.8 %collective-permute-start.6 = (bf16[1,72,256]{2,1,0:T(8,128)(2,1)S(1)}, bf16[1,72,256]{2,1,0:T(8,128)(2,1)S(1)}, u32[]{:S(2)}, u32[]{:S(2)}) collective-permute-start(bf16[1,72,256]{2,1,0:T(8,128)(2,1)S(1)} %get-tuple-element.17), channel_id=1, source_target_pairs={{0,6},{1,7},{2,4},{3,5},{4,2},{5,3},{6,0},{7,1},{8,14},{9,15},{10,... | collective-permute-start | bytes 110600 | tf_op jit(solution)/shard_map/ppermute | solution.py:24
  42.4 4.9 %collective-permute-start.5 = (bf16[1,72,256]{2,1,0:T(8,128)(2,1)S(1)}, bf16[1,72,256]{2,1,0:T(8,128)(2,1)S(1)}, u32[]{:S(2)}, u32[]{:S(2)}) collective-permute-start(bf16[1,72,256]{2,1,0:T(8,128)(2,1)S(1)} %get-tuple-element.18), channel_id=1, source_target_pairs={{0,4},{1,5},{2,6},{3,7},{4,0},{5,1},{6,2},{7,3},{8,12},{9,13},{10,... | collective-permute-start | bytes 110600 | tf_op jit(solution)/shard_map/ppermute | solution.py:24

commit v2 on v1

--- a/solution.py
+++ b/solution.py
@@ -22,6 +22,10 @@
 def xor_permute(value, mask):
     count = lax.axis_size(ALL)
     return lax.ppermute(value, ALL, [(i, i ^ mask) for i in range(count)])
+
+
+def padded(rows):
+    return -(-rows // CODE_ROWS) * CODE_ROWS
 
 
 def stage_plan(size_ja, size_ka):
@@ -47,6 +51,7 @@
     factor_sems,
     coords,
     count,
+    codes,
     waiting,
     first,
     second,
@@ -54,7 +59,7 @@
     edge, rank = c_ref.shape[1:]
     third_dev = c_ref.shape[0]
     low_bits = (third_dev - 1).bit_length()
-    half = keep_ref.shape[0]
+    half = codes.shape[0] // 2
     device = lax.axis_index(ALL)
 
     def fetch(slot):
@@ -70,6 +75,9 @@
         copy.start()
     fetch(0).start()
 
+    keep_ref[...] = jnp.zeros_like(keep_ref)
+    send_ref[...] = jnp.zeros_like(send_ref)
+    codes[...] = jnp.zeros_like(codes)
     for cell in range(waiting.shape[0]):
         waiting[cell] = -1
     copies[0].wait()
@@ -105,28 +113,24 @@
         def _():
             fetch_pass(index)
 
-    keep_ref[...] = jnp.zeros_like(keep_ref)
-    send_ref[...] = jnp.zeros_like(send_ref)
     for copy in copies[2:]:
         copy.wait()
-    lanes = lax.broadcasted_iota(jnp.int32, (CODE_ROWS, rank), 1)
+    lanes = lax.broadcasted_iota(jnp.int32, (1, rank), 1)
 
     def put(slot, code, term):
         relative = jnp.bitwise_xor(coords[0, slot], device)
         target = 0
         for new_bit, old_bit in enumerate(order):
             target += (lax.shift_right_logical(relative, old_bit) & 1) << new_bit
-        row_code = jnp.where(lanes == relative, code, 0.0).astype(jnp.bfloat16)
+        codes[pl.ds(target, 1), :] = jnp.where(lanes == relative, code, 0.0)
 
         @pl.when(target < half)
         def _():
-            keep_ref[target, :edge] = term
-            keep_ref[target, edge:] = row_code
+            keep_ref[pl.ds(pl.multiple_of(target * edge, edge), edge), :] = term
 
         @pl.when(target >= half)
         def _():
-            send_ref[target - half, :edge] = term
-            send_ref[target - half, edge:] = row_code
+            send_ref[pl.ds(pl.multiple_of((target - half) * edge, edge), edge), :] = term
 
     def step(index, carry):
         @pl.when(index + AHEAD < passes)
@@ -161,12 +165,14 @@
         return carry
 
     lax.fori_loop(0, passes, step, 0)
+    keep_ref[half * edge : half * edge + half, :] = codes[:half].astype(jnp.bfloat16)
+    send_ref[half * edge : half * edge + half, :] = codes[half:].astype(jnp.bfloat16)
 
 
 def own_terms(order, blocks, b_blocks, c_blocks, coords, count, total_rows):
     slots, edge, width = blocks.shape
     rank = b_blocks.shape[2]
-    half = jax.ShapeDtypeStruct((total_rows // 2, edge + CODE_ROWS, rank), jnp.bfloat16)
+    half = jax.ShapeDtypeStruct((total_rows // 2 * edge + padded(total_rows // 2), rank), jnp.bfloat16)
     vmem = pl.BlockSpec(memory_space=pltpu.VMEM)
     hbm = pl.BlockSpec(memory_space=pltpu.HBM)
     in_hbm = functools.partial(pltpu.with_memory_space_constraint, memory_space=pltpu.HBM)
@@ -183,6 +189,7 @@
             pltpu.SemaphoreType.DMA((4,)),
             pltpu.SMEM((3, slots), jnp.int32),
             pltpu.SMEM((1,), jnp.int32),
+            pltpu.VMEM((total_rows, rank), jnp.float32),
             pltpu.SMEM((b_blocks.shape[0] * c_blocks.shape[0],), jnp.int32),
             pltpu.SMEM((slots,), jnp.int32),
             pltpu.SMEM((slots,), jnp.int32),
@@ -238,8 +245,8 @@
     return high, middle, (rest - middle.astype(jnp.float32)).astype(jnp.bfloat16)
 
 
-def solve_kernel(shape, moment_ref, gram_b, gram_c, out_ref, system, parts, work, b_list, c_list):
-    size_ja, size_ka, second_dev, third_dev, b_place, c_place = shape
+def solve_kernel(shape, moment_ref, gram_b, early_c, late_c, out_ref, system, parts, work, b_list, c_list):
+    size_ja, size_ka, second_dev, third_dev, b_place, c_place, last = shape
     edge, rank = out_ref.shape
     sources = size_ja * size_ka
     lanes = lax.broadcasted_iota(jnp.int32, (1, rank), 1)
@@ -255,27 +262,33 @@
         for group in range(pl.cdiv(sources, per))
     ]
     half = third_dev // 2
-    live = 0
+    live = [0, 0]
     for source in range(sources):
+        number, offset = c_place[source % size_ka]
+        late = int(number == last)
         code = lax.shift_right_logical(packed[source // per], width * (source % per)) & ((1 << width) - 1)
         field = lax.shift_right_logical(code, 1)
         second, third = lax.shift_right_logical(field, low_bits), field & ((1 << low_bits) - 1)
         upper = (third >= half).astype(jnp.int32)
         far = jnp.bitwise_xor(upper, core)
-        b_list[live] = b_place[source // size_ka] * second_dev + second
-        c_list[live] = (far * size_ka + c_place[source % size_ka]) * half + third - upper * half
-        live = live + (code & 1)
+        block = (0 if late else number) * 2 * third_dev + (far * 2 + offset) * half + third - upper * half
+        b_list[late, live[late]] = b_place[source // size_ka] * second_dev + second
+        c_list[late, live[late]] = block
+        live[late] = live[late] + (code & 1)
 
     strip = min(STRIP, rank)
     for low in range(0, rank, strip):
         rows = lax.broadcasted_iota(jnp.int32, (strip, rank), 0) + low
         columns = lax.broadcasted_iota(jnp.int32, (strip, rank), 1)
 
-        def add(index, total, low=low):
-            left = gram_b[b_list[index], low : low + strip, :]
-            return total + left * gram_c[c_list[index], low : low + strip, :]
-
-        total = lax.fori_loop(0, live, add, jnp.where(rows == columns, RIDGE, 0.0))
+        total = jnp.where(rows == columns, RIDGE, 0.0)
+        for late, gram_c in enumerate((early_c, late_c)):
+
+            def add(index, total, late=late, gram_c=gram_c, low=low):
+                left = gram_b[b_list[late, index], low : low + strip, :]
+                return total + left * gram_c[c_list[late, index], low : low + strip, :]
+
+            total = lax.fori_loop(0, live[late], add, total)
         system[low : low + strip] = total
         for place, part in enumerate(split3(total)):
             parts[place, low : low + strip] = part
@@ -351,20 +364,20 @@
     return pl.pallas_call(
         functools.partial(solve_kernel, shape),
         out_shape=jax.ShapeDtypeStruct((edge, rank), jnp.float32),
-        in_specs=[vmem, vmem, vmem],
+        in_specs=[vmem] * 4,
         out_specs=vmem,
         scratch_shapes=[
             pltpu.VMEM((rank, rank), jnp.float32),
             pltpu.VMEM((3, rank, rank), jnp.bfloat16),
             pltpu.VMEM((rank + edge, rank), jnp.float32),
-            pltpu.SMEM((sources + 1,), jnp.int32),
-            pltpu.SMEM((sources + 1,), jnp.int32),
+            pltpu.SMEM((2, sources + 1), jnp.int32),
+            pltpu.SMEM((2, sources + 1), jnp.int32),
         ],
         compiler_params=pltpu.CompilerParams(
-            vmem_limit_bytes=(gram_b.size + gram_c.size) * 4 + 8 * MIB
+            vmem_limit_bytes=(gram_b.size + sum(c.size for c in gram_c)) * 4 + 8 * MIB
         ),
         name="solve",
-    )(moment, gram_b, gram_c)
+    )(moment, gram_b, *gram_c)
 
 
 def body(blocks, factor_b, factor_c, block_coords, block_count):
@@ -389,36 +402,46 @@
         held = held + [q ^ (1 << bit) for q in held]
     for place, q in enumerate(held):
         b_place[q] = place
-    c_half = lax.dynamic_slice_in_dim(c_blocks, core * (third_dev // 2), third_dev // 2, 0)
-    c_place, held = [0] * size_ka, [0]
-    top = size_ka.bit_length() - 2
-    for group in [[0]] + [[bit] for bit in range(top, 0, -1)]:
-        masks = [sum(1 << bit for i, bit in enumerate(group) if piece >> i & 1) for piece in range(1 << len(group))]
-        arrived = [c_half]
-        for piece, mask in enumerate(masks[1:], 1):
-            arrived.append(xor_permute(c_half, mask))
-        c_half = jnp.concatenate(arrived, axis=0)
-        held = [q ^ mask for mask in masks for q in held]
-    for place, q in enumerate(held):
-        c_place[q] = place
-    c_other = xor_permute(c_half, core_mask)
+    c_place = [0] * size_ka
+    c_near = xor_permute(c_blocks, 1)
+    halves = [lax.dynamic_slice_in_dim(c, core * (third_dev // 2), third_dev // 2, 0) for c in (c_blocks, c_near)]
+    c_sets = [jnp.concatenate(halves, axis=0)]
+    starts = [0]
+    for bit in range(size_ka.bit_length() - 2, 0, -1):
+        for number in range(len(c_sets)):
+            c_sets.append(xor_permute(c_sets[number], 1 << bit))
+        starts = starts + [q ^ (1 << bit) for q in starts]
+    for number, q in enumerate(starts):
+        c_place[q], c_place[q ^ 1] = (number, 0), (number, 1)
+    c_other = []
+    for number, part in enumerate(c_sets):
+        c_other.append(xor_permute(part, core_mask))
     gram_b = grams_of(b_parts)
-    gram_c = grams_of([c_half, c_other])
+    c_pairs = [[part, other] for part, other in zip(c_sets, c_other)]
+    gram_c = [grams_of(sum(c_pairs[:-1], []))]
+    gram_c.append(grams_of(c_pairs[-1]))
 
     keep, send = own_terms(order, blocks, b_blocks, c_blocks, block_coords, block_count, devices)
     received = xor_permute(send, core_mask)
     total = keep.astype(jnp.float32) + received.astype(jnp.float32)
+    rows = devices // 2
     for group in plan[1:]:
-        pieces = total.reshape((1 << len(group), -1) + total.shape[1:])
-        total = pieces[0]
+        rows >>= len(group)
+        number = 1 << len(group)
+        terms = [total[rows * edge * piece : rows * edge * (piece + 1)] for piece in range(number)]
+        first_code = rows * number * edge
+        codes = [total[first_code + rows * piece : first_code + rows * (piece + 1)] for piece in range(number)]
+        spare = ((0, padded(rows) - rows), (0, 0))
+        messages = [jnp.concatenate([part, jnp.pad(code, spare)], axis=0) for part, code in zip(terms, codes)]
         arrived = []
-        for piece in range(1, 1 << len(group)):
+        for piece in range(1, number):
             mask = sum(1 << bit for i, bit in enumerate(group) if piece >> i & 1)
-            arrived.append(xor_permute(pieces[piece].astype(jnp.bfloat16), mask))
+            arrived.append(xor_permute(messages[piece].astype(jnp.bfloat16), mask))
+        total = messages[0]
         for part in arrived:
             total = total + part.astype(jnp.float32)
-    shape = (size_ja, size_ka, second_dev, third_dev, tuple(b_place), tuple(c_place))
-    return solve(shape, total[0], gram_b, gram_c, edge)
+    shape = (size_ja, size_ka, second_dev, third_dev, tuple(b_place), tuple(c_place), len(c_sets) - 1)
+    return solve(shape, total, gram_b, gram_c, edge)
 
 
 def solution(mesh):

time: 54.4 us -> 55.9 us (1.028)
  starting transfers between devices: 9.17 us -> 12 us
  waiting for transfers between devices: 20.9 us -> 19.3 us
    ppermute x14 -> x18, starting transfers between devices: 9.17 us -> 12 us  [xor_permute(): return lax.ppermute(value, ALL, [(i, i ^ mask) for i in range(count)])]
    ppermute x14 -> x18, waiting for transfers between devices: 20.9 us -> 19.3 us  [xor_permute(): return lax.ppermute(value, ALL, [(i, i ^ mask) for i in range(count)])]
    pallas_call x2 -> x3, Pallas kernels: 2.59 us -> 2.79 us  [grams_of(): pl.pallas_call(grams_kernel, out_shape=jax.ShapeDtypeStruct((number, rank...]
  transfers between devices with their start and end apart: 14 -> 18, of which waited for: 8 -> 4; matrix products, arithmetic and copies ran while one was open for 1% -> 1% of each run, Pallas kernels for 2% -> 5%
where the time goes in v2:
time: 55.9 us; the launch traced here: 55.7 us
  Pallas kernels  23.1 us (41%)
  waiting for transfers between devices  19.3 us (35%)
  starting transfers between devices  12 us (21%)
  between operations  0.92 us (2%)
    ppermute x18, waiting for transfers between devices, xor_permute(): return lax.ppermute(value, ALL, [(i, i ^ mask) for i in range(count)])  19.3 us
    pallas_call x1, Pallas kernels, own_terms(): pl.pallas_call(functools.partial(terms_kernel, order), out_shape=(half, h...  14.7 us
    ppermute x18, starting transfers between devices, xor_permute(): return lax.ppermute(value, ALL, [(i, i ^ mask) for i in range(count)])  12 us
    pallas_call x1, Pallas kernels, solve(): pl.pallas_call(functools.partial(solve_kernel, shape), out_shape=jax.Shap...  5.68 us
    pallas_call x3, Pallas kernels, grams_of(): pl.pallas_call(grams_kernel, out_shape=jax.ShapeDtypeStruct((number, rank...  2.79 us
  transfers between devices with their start and end apart: 18, of which 4 were waited for; matrix products, arithmetic and copies ran while one was open for 1% of the time, Pallas kernels for 5%

profile of v2, /device:TPU:0, one launch (start us, length us, event | category | flops | bytes accessed | tf_op | source)
XLA Modules:
  0.0 55.7 jit_solution(5865328777097112257)
XLA Ops:
  0.7 0.0 copy-start.1
  0.7 0.0 copy-start
  0.7 14.7 %own_terms.1 = (bf16[1040,256]{1,0:T(8,128)(2,1)S(1)}, bf16[1040,256]{1,0:T(8,128)(2,1)S(1)}) custom-call(s32[3,32]{1,0:T(4,128)} %bitcast.10, s32[1]{0:T(128)S(6)} %copy.6.count_hbm, bf16[32,64,4096]{2,1,0:T(8,128)(2,1)} %blocks.1, bf16[8,64,256]{2,1,0:T(8,128)(2,1)} %bitcast.3, bf16[4,64,256]{2,1,0:T(8,128)(2,1)} %bitcast.7), custom_call_target="tpu_custom_call" | custom-call | flops 4294967296 | bytes 16777216 | tf_op jit(solution)/shard_map/own_terms/pallas_call | solution.py:179
  15.3 0.1 collective-permute-start
  15.4 0.0 copy-done.1
  15.4 0.3 collective-permute-start.10
  15.7 0.0 copy-done
  15.7 1.1 %collective-permute-start.7 = (bf16[8,64,256]{2,1,0:T(8,128)(2,1)S(1)}, bf16[8,64,256]{2,1,0:T(8,128)(2,1)S(1)}, u32[]{:S(2)}, u32[]{:S(2)}) collective-permute-start(bf16[8,64,256]{2,1,0:T(8,128)(2,1)S(1)} %bitcast.4), channel_id=1, source_target_pairs={{0,16},{1,17},{2,18},{3,19},{4,20},{5,21},{6,22},{7,23},{8,24},{9,... | collective-permute-start | bytes 786440 | tf_op jit(solution)/shard_map/ppermute | solution.py:24
  16.8 4.5 %collective-permute-done.10 = bf16[4,64,256]{2,1,0:T(8,128)(2,1)S(1)} collective-permute-done((bf16[4,64,256]{2,1,0:T(8,128)(2,1)S(1)}, bf16[4,64,256]{2,1,0:T(8,128)(2,1)S(1)}, u32[]{:S(2)}, u32[]{:S(2)}) %collective-permute-start.10) | collective-permute-done | bytes 131104 | tf_op jit(solution)/shard_map/ppermute | solution.py:24
  21.3 0.0 collective-permute-done
  21.3 0.1 convert_add_fusion
  21.5 1.0 %collective-permute-start.3 = (bf16[264,256]{1,0:T(8,128)(2,1)S(1)}, bf16[264,256]{1,0:T(8,128)(2,1)S(1)}, u32[]{:S(2)}, u32[]{:S(2)}) collective-permute-start(bf16[264,256]{1,0:T(8,128)(2,1)S(1)} %fusion.8), channel_id=1, source_target_pairs={{0,17},{1,16},{2,19},{3,18},{4,21},{5,20},{6,23},{7,22},{8,25},{9,... | collective-permute-start | bytes 405512 | tf_op jit(solution)/shard_map/ppermute | solution.py:24
  22.5 1.8 %collective-permute-start.2 = (bf16[264,256]{1,0:T(8,128)(2,1)S(1)}, bf16[264,256]{1,0:T(8,128)(2,1)S(1)}, u32[]{:S(2)}, u32[]{:S(2)}) collective-permute-start(bf16[264,256]{1,0:T(8,128)(2,1)S(1)} %fusion.7), channel_id=1, source_target_pairs={{0,1},{1,0},{2,3},{3,2},{4,5},{5,4},{6,7},{7,6},{8,9},{9,8},{10,11... | collective-permute-start | bytes 405512 | tf_op jit(solution)/shard_map/ppermute | solution.py:24
  24.3 0.9 %collective-permute-start.1 = (bf16[264,256]{1,0:T(8,128)(2,1)S(1)}, bf16[264,256]{1,0:T(8,128)(2,1)S(1)}, u32[]{:S(2)}, u32[]{:S(2)}) collective-permute-start(bf16[264,256]{1,0:T(8,128)(2,1)S(1)} %fusion.6), channel_id=1, source_target_pairs={{0,16},{1,17},{2,18},{3,19},{4,20},{5,21},{6,22},{7,23},{8,24},{9,... | collective-permute-start | bytes 405512 | tf_op jit(solution)/shard_map/ppermute | solution.py:24
  25.3 0.1 collective-permute-start.12
  25.4 0.0 collective-permute-done.7.refs_1_
  25.4 0.1 collective-permute-start.8
  25.5 8.5 %collective-permute-done.12.refs_2_ = bf16[4,64,256]{2,1,0:T(8,128)(2,1)S(1)} collective-permute-done((bf16[4,64,256]{2,1,0:T(8,128)(2,1)S(1)}, bf16[4,64,256]{2,1,0:T(8,128)(2,1)S(1)}, u32[]{:S(2)}, u32[]{:S(2)}) %collective-permute-start.12) | collective-permute-done | bytes 131104 | tf_op jit(solution)/shard_map/ppermute | solution.py:24
  33.9 0.0 collective-permute-start.11
  33.9 0.0 collective-permute-done.3
  33.9 0.1 collective-permute-start.14
  34.0 0.0 collective-permute-done.2
  34.0 0.5 collective-permute-start.9
  34.5 0.0 collective-permute-done.1
  34.5 1.7 %collective-permute-start.16 = (bf16[4,64,256]{2,1,0:T(8,128)(2,1)S(1)}, bf16[4,64,256]{2,1,0:T(8,128)(2,1)S(1)}, u32[]{:S(2)}, u32[]{:S(2)}) collective-permute-start(bf16[4,64,256]{2,1,0:T(8,128)(2,1)S(1)} %collective-permute-done.12.refs_2_), channel_id=1, source_target_pairs={{0,2},{1,3},{2,0},{3,1},{4,6},{5,7},{6,4},{7,5},{8,10},{9,11},{10,... | collective-permute-start | bytes 393224 | tf_op jit(solution)/shard_map/ppermute | solution.py:24
  36.2 0.1 fusion.19
  36.3 0.0 collective-permute-done.11.refs_1_
  36.3 0.1 collective-permute-start.13
  36.4 3.9 %collective-permute-done.14.refs_4_ = bf16[4,64,256]{2,1,0:T(8,128)(2,1)S(1)} collective-permute-done((bf16[4,64,256]{2,1,0:T(8,128)(2,1)S(1)}, bf16[4,64,256]{2,1,0:T(8,128)(2,1)S(1)}, u32[]{:S(2)}, u32[]{:S(2)}) %collective-permute-start.14) | collective-permute-done | bytes 131104 | tf_op jit(solution)/shard_map/ppermute | solution.py:24
  40.3 0.0 collective-permute-start.15
  40.3 2.3 %collective-permute-done.16.refs_0_ = bf16[4,64,256]{2,1,0:T(8,128)(2,1)S(1)} collective-permute-done((bf16[4,64,256]{2,1,0:T(8,128)(2,1)S(1)}, bf16[4,64,256]{2,1,0:T(8,128)(2,1)S(1)}, u32[]{:S(2)}, u32[]{:S(2)}) %collective-permute-start.16) | collective-permute-done | bytes 131104 | tf_op jit(solution)/shard_map/ppermute | solution.py:24
  42.7 0.0 collective-permute-start.17
  42.7 0.0 collective-permute-done.13.refs_3_
  42.7 0.5 collective-permute-start.6
  43.2 0.0 collective-permute-done.15.refs_5_
  43.2 1.3 %collective-permute-start.5 = (bf16[72,256]{1,0:T(8,128)(2,1)S(1)}, bf16[72,256]{1,0:T(8,128)(2,1)S(1)}, u32[]{:S(2)}, u32[]{:S(2)}) collective-permute-start(bf16[72,256]{1,0:T(8,128)(2,1)S(1)} %fusion.16), channel_id=1, source_target_pairs={{0,4},{1,5},{2,6},{3,7},{4,0},{5,1},{6,2},{7,3},{8,12},{9,13},{10,... | collective-permute-start | bytes 110600 | tf_op jit(solution)/shard_map/ppermute | solution.py:24
  44.5 0.0 collective-permute-done.17.refs_1_
  44.5 2.6 %collective-permute-start.4 = (bf16[72,256]{1,0:T(8,128)(2,1)S(1)}, bf16[72,256]{1,0:T(8,128)(2,1)S(1)}, u32[]{:S(2)}, u32[]{:S(2)}) collective-permute-start(bf16[72,256]{1,0:T(8,128)(2,1)S(1)} %fusion.15), channel_id=1, source_target_pairs={{0,2},{1,3},{2,0},{3,1},{4,6},{5,7},{6,4},{7,5},{8,10},{9,11},{10,... | collective-permute-start | bytes 110600 | tf_op jit(solution)/shard_map/ppermute | solution.py:24
  47.2 1.0 %grams.4.early_c = f32[24,256,256]{2,1,0:T(8,128)S(1)} custom-call(bf16[4,64,256]{2,1,0:T(8,128)(2,1)S(1)} %pad_maximum_fusion.refs_0_, bf16[4,64,256]{2,1,0:T(8,128)(2,1)S(1)} %collective-permute-done.11.refs_1_, bf16[4,64,256]{2,1,0:T(8,128)(2,1)S(1)} %collective-permute-done.12.refs_2_, bf16[4,64,256]{2,1,0:T(8,128)(2,1)S(1)} %collective-permute-done.13.refs_3_, ...), custom_call_target="tpu_custom_call" | custom-call | flops 201326592 | bytes 786432 | tf_op jit(solution)/shard_map/grams/pallas_call | solution.py:226
  48.2 0.5 grams.5.late_c
  48.7 0.0 collective-permute-done.8.refs_2_
  48.7 0.0 collective-permute-done.9.refs_3_
  48.7 1.3 %grams.3.gram_b = f32[32,256,256]{2,1,0:T(8,128)S(1)} custom-call(bf16[8,64,256]{2,1,0:T(8,128)(2,1)S(1)} %bitcast.6, bf16[8,64,256]{2,1,0:T(8,128)(2,1)S(1)} %collective-permute-done.7.refs_1_, bf16[8,64,256]{2,1,0:T(8,128)(2,1)S(1)} %collective-permute-done.8.refs_2_, bf16[8,64,256]{2,1,0:T(8,128)(2,1)S(1)} %collective-permute-done.9.refs_3_), custom_call_target="tpu_custom_call" | custom-call | flops 268435456 | bytes 1048576 | tf_op jit(solution)/shard_map/grams/pallas_call | solution.py:226
  50.0 0.0 collective-permute-done.6
  50.0 0.0 collective-permute-done.5
  50.0 0.0 collective-permute-done.4
  50.1 5.7 %solve.1 = f32[64,256]{1,0:T(8,128)} custom-call(f32[72,256]{1,0:T(8,128)S(1)} %fusion.11.moment_ref, f32[32,256,256]{2,1,0:T(8,128)S(1)} %grams.3.gram_b, f32[24,256,256]{2,1,0:T(8,128)S(1)} %grams.4.early_c, f32[8,256,256]{2,1,0:T(8,128)S(1)} %grams.5.late_c), custom_call_target="tpu_custom_call" | custom-call | tf_op jit(solution)/shard_map/solve/pallas_call | solution.py:364
  (18 shorter events, 0.2 us)
Async XLA Ops:
  0.7 14.8 %copy-start.1 = (bf16[256,256]{1,0:T(8,128)(2,1)S(1)}, bf16[256,256]{1,0:T(8,128)(2,1)}, u32[]{:S(2)}) copy-start(bf16[256,256]{1,0:T(8,128)(2,1)} %param.7) | copy-start | bytes 393220
  0.7 15.0 %copy-start = (bf16[512,256]{1,0:T(8,128)(2,1)S(1)}, bf16[512,256]{1,0:T(8,128)(2,1)}, u32[]{:S(2)}) copy-start(bf16[512,256]{1,0:T(8,128)(2,1)} %param.6) | copy-start | bytes 786436
  15.3 6.0 %collective-permute-start = (bf16[1040,256]{1,0:T(8,128)(2,1)S(1)}, bf16[1040,256]{1,0:T(8,128)(2,1)S(1)}, u32[]{:S(2)}, u32[]{:S(2)}) collective-permute-start(bf16[1040,256]{1,0:T(8,128)(2,1)S(1)} %get-tuple-element.8), channel_id=1, source_target_pairs={{0,8},{1,9},{2,10},{3,11},{4,12},{5,13},{6,14},{7,15},{8,0},{9,1},... | collective-permute-start | bytes 1597448 | tf_op jit(solution)/shard_map/ppermute | solution.py:24
  15.4 5.9 %collective-permute-start.10 = (bf16[4,64,256]{2,1,0:T(8,128)(2,1)S(1)}, bf16[4,64,256]{2,1,0:T(8,128)(2,1)S(1)}, u32[]{:S(2)}, u32[]{:S(2)}) collective-permute-start(bf16[4,64,256]{2,1,0:T(8,128)(2,1)S(1)} %bitcast.8), channel_id=1, source_target_pairs={{0,1},{1,0},{2,3},{3,2},{4,5},{5,4},{6,7},{7,6},{8,9},{9,8},{10,11... | collective-permute-start | bytes 393224 | tf_op jit(solution)/shard_map/ppermute | solution.py:24
  15.7 9.7 %collective-permute-start.7 = (bf16[8,64,256]{2,1,0:T(8,128)(2,1)S(1)}, bf16[8,64,256]{2,1,0:T(8,128)(2,1)S(1)}, u32[]{:S(2)}, u32[]{:S(2)}) collective-permute-start(bf16[8,64,256]{2,1,0:T(8,128)(2,1)S(1)} %bitcast.4), channel_id=1, source_target_pairs={{0,16},{1,17},{2,18},{3,19},{4,20},{5,21},{6,22},{7,23},{8,24},{9,... | collective-permute-start | bytes 786440 | tf_op jit(solution)/shard_map/ppermute | solution.py:24
  21.5 12.4 %collective-permute-start.3 = (bf16[264,256]{1,0:T(8,128)(2,1)S(1)}, bf16[264,256]{1,0:T(8,128)(2,1)S(1)}, u32[]{:S(2)}, u32[]{:S(2)}) collective-permute-start(bf16[264,256]{1,0:T(8,128)(2,1)S(1)} %fusion.8), channel_id=1, source_target_pairs={{0,17},{1,16},{2,19},{3,18},{4,21},{5,20},{6,23},{7,22},{8,25},{9,... | collective-permute-start | bytes 405512 | tf_op jit(solution)/shard_map/ppermute | solution.py:24
  22.5 11.5 %collective-permute-start.2 = (bf16[264,256]{1,0:T(8,128)(2,1)S(1)}, bf16[264,256]{1,0:T(8,128)(2,1)S(1)}, u32[]{:S(2)}, u32[]{:S(2)}) collective-permute-start(bf16[264,256]{1,0:T(8,128)(2,1)S(1)} %fusion.7), channel_id=1, source_target_pairs={{0,1},{1,0},{2,3},{3,2},{4,5},{5,4},{6,7},{7,6},{8,9},{9,8},{10,11... | collective-permute-start | bytes 405512 | tf_op jit(solution)/shard_map/ppermute | solution.py:24
  24.3 10.2 %collective-permute-start.1 = (bf16[264,256]{1,0:T(8,128)(2,1)S(1)}, bf16[264,256]{1,0:T(8,128)(2,1)S(1)}, u32[]{:S(2)}, u32[]{:S(2)}) collective-permute-start(bf16[264,256]{1,0:T(8,128)(2,1)S(1)} %fusion.6), channel_id=1, source_target_pairs={{0,16},{1,17},{2,18},{3,19},{4,20},{5,21},{6,22},{7,23},{8,24},{9,... | collective-permute-start | bytes 405512 | tf_op jit(solution)/shard_map/ppermute | solution.py:24
  25.3 8.7 %collective-permute-start.12 = (bf16[4,64,256]{2,1,0:T(8,128)(2,1)S(1)}, bf16[4,64,256]{2,1,0:T(8,128)(2,1)S(1)}, u32[]{:S(2)}, u32[]{:S(2)}) collective-permute-start(bf16[4,64,256]{2,1,0:T(8,128)(2,1)S(1)} %pad_maximum_fusion.refs_0_), channel_id=1, source_target_pairs={{0,4},{1,5},{2,6},{3,7},{4,0},{5,1},{6,2},{7,3},{8,12},{9,13},{10,... | collective-permute-start | bytes 393224 | tf_op jit(solution)/shard_map/ppermute | solution.py:24
  25.4 23.3 %collective-permute-start.8 = (bf16[8,64,256]{2,1,0:T(8,128)(2,1)S(1)}, bf16[8,64,256]{2,1,0:T(8,128)(2,1)S(1)}, u32[]{:S(2)}, u32[]{:S(2)}) collective-permute-start(bf16[8,64,256]{2,1,0:T(8,128)(2,1)S(1)} %bitcast.5), channel_id=1, source_target_pairs={{0,8},{1,9},{2,10},{3,11},{4,12},{5,13},{6,14},{7,15},{8,0},{9,1},... | collective-permute-start | bytes 786440 | tf_op jit(solution)/shard_map/ppermute | solution.py:24
  33.9 2.4 %collective-permute-start.11 = (bf16[4,64,256]{2,1,0:T(8,128)(2,1)S(1)}, bf16[4,64,256]{2,1,0:T(8,128)(2,1)S(1)}, u32[]{:S(2)}, u32[]{:S(2)}) collective-permute-start(bf16[4,64,256]{2,1,0:T(8,128)(2,1)S(1)} %pad_maximum_fusion.refs_0_), channel_id=1, source_target_pairs={{0,8},{1,9},{2,10},{3,11},{4,12},{5,13},{6,14},{7,15},{8,0},{9,1},... | collective-permute-start | bytes 393224 | tf_op jit(solution)/shard_map/ppermute | solution.py:24
  33.9 6.4 %collective-permute-start.14 = (bf16[4,64,256]{2,1,0:T(8,128)(2,1)S(1)}, bf16[4,64,256]{2,1,0:T(8,128)(2,1)S(1)}, u32[]{:S(2)}, u32[]{:S(2)}) collective-permute-start(bf16[4,64,256]{2,1,0:T(8,128)(2,1)S(1)} %pad_maximum_fusion.refs_0_), channel_id=1, source_target_pairs={{0,2},{1,3},{2,0},{3,1},{4,6},{5,7},{6,4},{7,5},{8,10},{9,11},{10,... | collective-permute-start | bytes 393224 | tf_op jit(solution)/shard_map/ppermute | solution.py:24
  34.0 14.6 %collective-permute-start.9 = (bf16[8,64,256]{2,1,0:T(8,128)(2,1)S(1)}, bf16[8,64,256]{2,1,0:T(8,128)(2,1)S(1)}, u32[]{:S(2)}, u32[]{:S(2)}) collective-permute-start(bf16[8,64,256]{2,1,0:T(8,128)(2,1)S(1)} %collective-permute-done.7.refs_1_), channel_id=1, source_target_pairs={{0,8},{1,9},{2,10},{3,11},{4,12},{5,13},{6,14},{7,15},{8,0},{9,1},... | collective-permute-start | bytes 786440 | tf_op jit(solution)/shard_map/ppermute | solution.py:24
  34.5 8.1 %collective-permute-start.16 = (bf16[4,64,256]{2,1,0:T(8,128)(2,1)S(1)}, bf16[4,64,256]{2,1,0:T(8,128)(2,1)S(1)}, u32[]{:S(2)}, u32[]{:S(2)}) collective-permute-start(bf16[4,64,256]{2,1,0:T(8,128)(2,1)S(1)} %collective-permute-done.12.refs_2_), channel_id=1, source_target_pairs={{0,2},{1,3},{2,0},{3,1},{4,6},{5,7},{6,4},{7,5},{8,10},{9,11},{10,... | collective-permute-start | bytes 393224 | tf_op jit(solution)/shard_map/ppermute | solution.py:24
  36.3 6.3 %collective-permute-start.13 = (bf16[4,64,256]{2,1,0:T(8,128)(2,1)S(1)}, bf16[4,64,256]{2,1,0:T(8,128)(2,1)S(1)}, u32[]{:S(2)}, u32[]{:S(2)}) collective-permute-start(bf16[4,64,256]{2,1,0:T(8,128)(2,1)S(1)} %collective-permute-done.12.refs_2_), channel_id=1, source_target_pairs={{0,8},{1,9},{2,10},{3,11},{4,12},{5,13},{6,14},{7,15},{8,0},{9,1},... | collective-permute-start | bytes 393224 | tf_op jit(solution)/shard_map/ppermute | solution.py:24
  40.3 2.9 %collective-permute-start.15 = (bf16[4,64,256]{2,1,0:T(8,128)(2,1)S(1)}, bf16[4,64,256]{2,1,0:T(8,128)(2,1)S(1)}, u32[]{:S(2)}, u32[]{:S(2)}) collective-permute-start(bf16[4,64,256]{2,1,0:T(8,128)(2,1)S(1)} %collective-permute-done.14.refs_4_), channel_id=1, source_target_pairs={{0,8},{1,9},{2,10},{3,11},{4,12},{5,13},{6,14},{7,15},{8,0},{9,1},... | collective-permute-start | bytes 393224 | tf_op jit(solution)/shard_map/ppermute | solution.py:24
  42.7 1.9 %collective-permute-start.17 = (bf16[4,64,256]{2,1,0:T(8,128)(2,1)S(1)}, bf16[4,64,256]{2,1,0:T(8,128)(2,1)S(1)}, u32[]{:S(2)}, u32[]{:S(2)}) collective-permute-start(bf16[4,64,256]{2,1,0:T(8,128)(2,1)S(1)} %collective-permute-done.16.refs_0_), channel_id=1, source_target_pairs={{0,8},{1,9},{2,10},{3,11},{4,12},{5,13},{6,14},{7,15},{8,0},{9,1},... | collective-permute-start | bytes 393224 | tf_op jit(solution)/shard_map/ppermute | solution.py:24
  42.7 7.3 %collective-permute-start.6 = (bf16[72,256]{1,0:T(8,128)(2,1)S(1)}, bf16[72,256]{1,0:T(8,128)(2,1)S(1)}, u32[]{:S(2)}, u32[]{:S(2)}) collective-permute-start(bf16[72,256]{1,0:T(8,128)(2,1)S(1)} %fusion.17), channel_id=1, source_target_pairs={{0,6},{1,7},{2,4},{3,5},{4,2},{5,3},{6,0},{7,1},{8,14},{9,15},{10,... | collective-permute-start | bytes 110600 | tf_op jit(solution)/shard_map/ppermute | solution.py:24
  43.2 6.8 %collective-permute-start.5 = (bf16[72,256]{1,0:T(8,128)(2,1)S(1)}, bf16[72,256]{1,0:T(8,128)(2,1)S(1)}, u32[]{:S(2)}, u32[]{:S(2)}) collective-permute-start(bf16[72,256]{1,0:T(8,128)(2,1)S(1)} %fusion.16), channel_id=1, source_target_pairs={{0,4},{1,5},{2,6},{3,7},{4,0},{5,1},{6,2},{7,3},{8,12},{9,13},{10,... | collective-permute-start | bytes 110600 | tf_op jit(solution)/shard_map/ppermute | solution.py:24
  44.5 5.5 %collective-permute-start.4 = (bf16[72,256]{1,0:T(8,128)(2,1)S(1)}, bf16[72,256]{1,0:T(8,128)(2,1)S(1)}, u32[]{:S(2)}, u32[]{:S(2)}) collective-permute-start(bf16[72,256]{1,0:T(8,128)(2,1)S(1)} %fusion.15), channel_id=1, source_target_pairs={{0,2},{1,3},{2,0},{3,1},{4,6},{5,7},{6,4},{7,5},{8,10},{9,11},{10,... | collective-permute-start | bytes 110600 | tf_op jit(solution)/shard_map/ppermute | solution.py:24
